TPU v7x, 128 devices: a whole 4x4x4 slice. The times are simulated.
128 devices in a mesh: emb: 4 (over x), row: 16 (over z, y), phase: 2 (over core).
Axes of the slice: x: 4, y: 4, z: 4, core: 2. Of those that a mesh axis runs over, the one named last changes fastest.
Arguments:
- item_table: bfloat16 [4096, 512], P('emb'), may hold values from -10 to 10
- item_owner: int32 [4, 2, 4096, 1], P('emb', 'phase', 'row'), may hold values from 0 to 3; in each aligned block of 256 rows (0 to 255, 256 to 511, ..., all dimensions but the last counted through in order) at most 128 rows name the same one
- item_slot: int32 [4, 2, 4096], P('emb', 'phase', 'row'), may hold values from 0 to 1023
- seq_lengths: int32 [4, 2, 2], P('emb'), may hold values from 1 to 3072, 4096 in all within a row
- row_grads: bfloat16 [4, 2, 4096, 512], P('emb', 'phase', 'row'), may hold values from -6 to 6
- proj_weight: bfloat16 [2, 512, 2048], P('phase'), may hold values from -2 to 2
- out_weight: bfloat16 [2, 512, 512], P('phase'), may hold values from -0.25 to 0.25
- final_gain: float32 [512], replicated, may hold values from 0.1 to 1.9
Outputs:
- sequence_states: bfloat16 [4, 2, 4096, 512], P('emb', 'phase', 'row')
- table_grad: float32 [4096, 512], P(('emb', 'row', 'phase'))
Inputs may be any that keep to these rules, and one draw needn't show every extreme that they name: `item_owner`: among the 256 tokens of one device, at most 128 name the same owner, and in every draw some device has an owner named by exactly 128 of its tokens. `seq_lengths`: the 2 lengths of one micro-batch of one group sum to 4096; neither is longer than 3072.
All inputs are finite; a program needn't handle non-finite values.
Results may differ from a plain program's by a relative error of at most 0.013.
Values may be sent and summed in bfloat16 or wider, within the bound.
A program may use at most 64 MiB of HBM per device.

v0:
```python
import jax
import jax.numpy as jnp
from jax import lax
from jax.sharding import PartitionSpec as P

HEADS = 4
HEAD_DIM = 128


norm_eps = 1e-05


def passed_along(shard, axis, by):
    count = lax.axis_size(axis)
    pairs = [(i, i + by) for i in range(count) if 0 <= i + by < count]
    return lax.ppermute(shard, axis, pairs)


def layer_norm(values):
    average = jnp.mean(values, axis=-1, keepdims=True)
    centered = values - average
    return centered * lax.rsqrt(jnp.mean(centered * centered, axis=-1, keepdims=True) + norm_eps)


def segment_of(positions, lengths):
    bounds = jnp.cumsum(lengths)[:-1]
    return jnp.sum((positions[:, None] >= bounds[None, :]).astype(jnp.int32), axis=1)


def attend_keys(query_rows, query_pos, query_seg, lengths, running, pieces):
    key_piece, value_piece = pieces
    key_count = key_piece.shape[0]
    key_pos = jnp.arange(key_count, dtype=jnp.int32)
    key_seg = segment_of(key_pos, lengths)
    visible = (key_pos[None, :] <= query_pos[:, None]) & (key_seg[None, :] == query_seg[:, None])
    query_heads = query_rows.reshape(query_rows.shape[0], HEADS, HEAD_DIM)
    key_heads = key_piece.reshape(key_count, HEADS, HEAD_DIM)
    value_heads = value_piece.reshape(key_count, HEADS, HEAD_DIM)
    scores = jnp.einsum("qhd,khd->hqk", query_heads, key_heads, preferred_element_type=jnp.float32)
    attn_weights = jnp.where(visible[None], jax.nn.silu(scores), 0.0).astype(jnp.bfloat16)
    update = jnp.einsum(
        "hqk,khd->qhd", attn_weights, value_heads, preferred_element_type=jnp.float32
    )
    return update.reshape(running.shape)


def hstu_layer(feed_rows, proj_weight, out_weight, lengths):
    count_rows = feed_rows.shape[0]
    normed = layer_norm(feed_rows.astype(jnp.float32)).astype(jnp.bfloat16)
    projected = jnp.dot(normed, proj_weight[0], preferred_element_type=jnp.float32)
    activated = jax.nn.silu(projected).astype(jnp.bfloat16)
    inner_width = HEADS * HEAD_DIM
    gate_rows = activated[:, :inner_width]
    value_rows = activated[:, inner_width : 2 * inner_width]
    query_rows = activated[:, 2 * inner_width : 3 * inner_width]
    key_rows = activated[:, 3 * inner_width :]
    query_pos = lax.axis_index("row") * count_rows + jnp.arange(count_rows, dtype=jnp.int32)
    query_seg = segment_of(query_pos, lengths)
    mixed_heads = attend_keys(
        query_rows,
        query_pos,
        query_seg,
        lengths,
        jnp.zeros((count_rows, inner_width), jnp.float32),
        (
            lax.all_gather(key_rows, "row", axis=0, tiled=True),
            lax.all_gather(value_rows, "row", axis=0, tiled=True),
        ),
    )
    gated = (layer_norm(mixed_heads) * gate_rows.astype(jnp.float32)).astype(jnp.bfloat16)
    branch = jnp.dot(gated, out_weight[0], preferred_element_type=jnp.float32)
    return feed_rows.astype(jnp.float32) + branch


def body(
    item_table, item_owner, item_slot, seq_lengths, row_grads, proj_weight, out_weight, final_gain
):
    parties = lax.axis_size("emb")
    owners = item_owner.reshape(-1)
    slot_ids = item_slot.reshape(-1)
    count_rows = owners.shape[0]
    model_width = item_table.shape[1]
    owned_rows = item_table.shape[0]
    capacity = max(16, 2 * count_rows // parties)
    onehot = (owners[:, None] == jnp.arange(parties, dtype=jnp.int32)[None, :]).astype(jnp.int32)
    places = jnp.sum((jnp.cumsum(onehot, axis=0) - onehot) * onehot, axis=1)
    request = jnp.full((parties, capacity), -1, jnp.int32).at[owners, places].set(slot_ids)
    grad_rows = row_grads.reshape(count_rows, model_width)
    outgoing = (
        jnp.zeros((parties, capacity, model_width), jnp.bfloat16).at[owners, places].set(grad_rows)
    )
    asked_slots = lax.all_to_all(request, "emb", split_axis=0, concat_axis=0, tiled=True)
    is_valid = asked_slots >= 0
    looked = jnp.take(item_table, jnp.maximum(asked_slots, 0), axis=0)
    looked = jnp.where(is_valid[..., None], looked, jnp.zeros_like(looked))
    returned = lax.all_to_all(looked, "emb", split_axis=0, concat_axis=0, tiled=True)
    incoming = None
    own_rows = returned[owners, places]
    other_rows = passed_along(own_rows, "phase", -1)
    phase_id = lax.axis_index("phase")
    is_first = phase_id == 0
    phase_inputs = [own_rows, other_rows, other_rows]
    carried = own_rows
    outputs = []
    for tick_index in range(3):
        feed_rows = jnp.where(is_first, phase_inputs[tick_index], carried)
        micro = jnp.clip(tick_index - phase_id, 0, 1)
        lengths = lax.dynamic_index_in_dim(seq_lengths[0], micro, 0, keepdims=False)
        residual_sum = hstu_layer(feed_rows, proj_weight, out_weight, lengths)
        plain_rows = residual_sum.astype(jnp.bfloat16)
        closing = (layer_norm(residual_sum) * final_gain).astype(jnp.bfloat16)
        outputs.append(jnp.where(is_first, plain_rows, closing))
        if tick_index < 2:
            carried = passed_along(plain_rows, "phase", 1)
    returned_first = passed_along(outputs[1], "phase", -1)
    final_rows = jnp.where(is_first, returned_first, outputs[2])
    sequence_states = final_rows.reshape(1, 1, count_rows, model_width)
    incoming = lax.all_to_all(outgoing, "emb", split_axis=0, concat_axis=0, tiled=True)
    flat_slots = asked_slots.reshape(-1)
    targets = jnp.where(flat_slots >= 0, flat_slots, owned_rows)
    partial_value = (
        jnp.zeros((owned_rows, model_width), jnp.float32)
        .at[targets]
        .add(incoming.reshape(-1, model_width).astype(jnp.float32), mode="drop")
    )
    table_grad = lax.psum_scatter(
        partial_value.astype(jnp.bfloat16), ("row", "phase"), scatter_dimension=0, tiled=True
    ).astype(jnp.float32)
    return (sequence_states, table_grad)


def solution(mesh):
    placed = (
        P("emb", None),
        P("emb", "phase", "row", None),
        P("emb", "phase", "row"),
        P("emb", None, None),
        P("emb", "phase", "row", None),
        P("phase", None, None),
        P("phase", None, None),
        P(),
    )
    return jax.shard_map(
        body,
        mesh=mesh,
        in_specs=placed,
        out_specs=(P("emb", "phase", "row", None), P(("emb", "row", "phase"), None)),
        check_vma=False,
    )
```

profile of v0, /device:TPU:0, one launch (start us, length us, event | category | flops | bytes accessed | tf_op | source)
XLA Modules:
  0.0 450.5 jit_solution(11198467036668883595)
XLA Ops:
  8.1 0.9 compare_convert_fusion
  8.9 1.2 reduce-window.16
  10.5 0.7 fusion.100
  11.2 0.7 or_select_fusion
  11.9 21.4 %scatter_fusion = s32[4,128]{1,0:T(4,128)S(1)} fusion(s32[4,128]{1,0:T(4,128)S(1)} %broadcast_in_dim.49, s32[256]{0:T(256)S(1)} %bitcast.173, s32[256]{0:T(256)} %bitcast.196), kind=kCustom, calls=%fused_computation.2 | custom fusion | bytes 5120 | tf_op jit(solution)/shard_map/scatter | solution.py:87
  33.3 9.5 %all_to_all.19 = s32[4,1,128]{2,1,0:T(1,128)S(1)} all-to-all(s32[4,1,128]{2,1,0:T(1,128)S(1)} %bitcast.172), channel_id=1, replica_groups=mesh['emb'=4,'row'=16,'phase'=2] {'emb'}, dimensions={0} | all-to-all | bytes 4096 | tf_op jit(solution)/shard_map/all_to_all | solution.py:92
  42.8 2.6 gather_fusion
  45.5 1.2 select_select_fusion
  46.7 10.7 %all_to_all.20 = bf16[4,128,512]{2,1,0:T(8,128)(2,1)S(1)} all-to-all(bf16[4,128,512]{2,1,0:T(8,128)(2,1)S(1)} %select_select_fusion), channel_id=1, replica_groups=mesh['emb'=4,'row'=16,'phase'=2] {'emb'}, dimensions={0} | all-to-all | bytes 1048576 | tf_op jit(solution)/shard_map/all_to_all | solution.py:96
  57.4 2.1 gather_fusion.1
  59.7 0.2 fusion.50
  59.9 0.9 multiply_convert_fusion.2
  60.8 1.0 copy-done.7
  61.8 0.9 slice_bitcast_fusion.2
  62.7 0.7 all-gather.9.cloned.1.call-update
  63.5 0.2 reduce-window.21
  64.2 3.8 fusion.21
  68.0 1.3 collective-permute-start
  69.3 45.6 %all-gather.7.cloned.1.call-done = bf16[4096,512]{1,0:T(8,128)(2,1)} async-done(((bf16[256,512]{1,0:T(8,128)(2,1)}), bf16[4096,512]{1,0:T(8,128)(2,1)}) %all-gather.7.cloned.1.call-update) | async-done | bytes 4194320 | tf_op jit(solution)/shard_map/all_gather | solution.py:67
  114.9 6.4 %copy.68 = bf16[4096,512]{0,1:T(8,128)(2,1)} copy(bf16[4096,512]{1,0:T(8,128)(2,1)} %all-gather.7.cloned.1.call-done) | data formatting | bytes 8388608 | tf_op jit(solution)/shard_map/reshape | solution.py:38
  121.3 46.9 %all-gather.9.cloned.1.call-done = bf16[4096,512]{1,0:T(8,128)(2,1)} async-done(((bf16[256,512]{1,0:T(8,128)(2,1)}), bf16[4096,512]{1,0:T(8,128)(2,1)}) %all-gather.9.cloned.1.call-update) | async-done | bytes 4194320 | tf_op jit(solution)/shard_map/all_gather | solution.py:66
  168.2 10.5 %fusion.112 = (f32[256]{0:T(256)S(1)}, f32[4,128,256]{2,1,0:T(8,128)S(1)}) fusion(bf16[4096,4,128]{0,2,1:T(8,128)(2,1)} %bitcast.177, pred[256,4096]{1,0:T(8,128)(4,1)} %get-tuple-element.23, bf16[32,4,8,128]{3,2,1,0:T(8,128)(2,1)} %get-tuple-element.16, bf16[4096,512]{1,0:T(8,128)(2,1)} %all-gather.9.cloned.1.call-done), kind=kOutput, calls=%fused_computation.167 | convolution fusion | flops 2172780288 | bytes 10224640 | tf_op jit(solution)/shard_map/hqk,khd->qhd/dot_general | solution.py:41
  178.8 1.0 copy.69
  179.8 1.5 fusion.36
  181.2 1.8 collective-permute-start.1
  183.0 0.9 collective-permute-done.1
  184.0 1.1 convert_reduce_fusion.1
  185.1 0.2 fusion.48
  185.3 0.9 multiply_convert_fusion.1
  186.2 1.0 copy-done.5
  187.2 0.9 slice_bitcast_fusion.1
  188.1 0.5 all-gather.13.cloned.1.call-update
  188.7 0.8 broadcast.425
  189.5 34.0 %scatter_fusion.1 = bf16[4,128,512]{2,1,0:T(8,128)(2,1)} fusion(bf16[4,128,512]{2,1,0:T(8,128)(2,1)} %broadcast.425, s32[256]{0:T(256)S(1)} %bitcast.174, bf16[256,512]{1,0:T(8,128)(2,1)S(1)} %bitcast.183), kind=kCustom, calls=%fused_computation.3 | custom fusion | bytes 788480 | tf_op jit(solution)/shard_map/scatter | solution.py:90
  223.5 4.6 %all-to-all-start.2 = ((bf16[4,128,512]{2,1,0:T(8,128)(2,1)}), bf16[4,128,512]{2,1,0:T(8,128)(2,1)}, u32[]{:S(2)}, u32[]{:S(2)}) async-start(bf16[4,128,512]{2,1,0:T(8,128)(2,1)} %scatter_fusion.1), calls=%async_computation.2 | async-start | bytes 1048576 | tf_op jit(solution)/shard_map/all_to_all | solution.py:118
  228.1 11.2 %all-gather.11.cloned.1.call-done = bf16[4096,512]{1,0:T(8,128)(2,1)} async-done(((bf16[256,512]{1,0:T(8,128)(2,1)}), bf16[4096,512]{1,0:T(8,128)(2,1)}) %all-gather.11.cloned.1.call-update) | async-done | bytes 4194320 | tf_op jit(solution)/shard_map/all_gather | solution.py:67
  239.3 6.4 %copy.70 = bf16[4096,512]{0,1:T(8,128)(2,1)} copy(bf16[4096,512]{1,0:T(8,128)(2,1)} %all-gather.11.cloned.1.call-done) | data formatting | bytes 8388608 | tf_op jit(solution)/shard_map/reshape | solution.py:38
  245.7 46.7 %all-gather.13.cloned.1.call-done = bf16[4096,512]{1,0:T(8,128)(2,1)} async-done(((bf16[256,512]{1,0:T(8,128)(2,1)}), bf16[4096,512]{1,0:T(8,128)(2,1)}) %all-gather.13.cloned.1.call-update) | async-done | bytes 4194320 | tf_op jit(solution)/shard_map/all_gather | solution.py:66
  292.5 10.4 %fusion.117 = (f32[256]{0:T(256)S(1)}, f32[4,128,256]{2,1,0:T(8,128)S(1)}) fusion(bf16[4096,4,128]{0,2,1:T(8,128)(2,1)} %bitcast.178, pred[256,4096]{1,0:T(8,128)(4,1)} %get-tuple-element.22, bf16[32,4,8,128]{3,2,1,0:T(8,128)(2,1)} %get-tuple-element.13, bf16[4096,512]{1,0:T(8,128)(2,1)} %all-gather.13.cloned.1.call-done), kind=kOutput, calls=%fused_computation.168 | convolution fusion | flops 2172780288 | bytes 10224640 | tf_op jit(solution)/shard_map/hqk,khd->qhd/dot_general | solution.py:41
  303.0 0.6 copy-done.3
  303.6 1.2 copy.71
  304.9 1.4 fusion.122
  306.3 0.2 multiply_reduce_fusion.1
  306.5 0.9 fusion.61
  307.4 1.6 collective-permute-start.3
  309.0 5.6 %scatter_custom_fusion.2 = f32[1024,512]{1,0:T(8,128)} fusion(s32[512]{0:T(512)S(1)} %bitcast.195, bf16[512,512]{1,0:T(8,128)(2,1)} %bitcast.39, f32[]{:T(128)} %constant.95.clone.1), kind=kCustom, calls=%fused_computation.37 | custom fusion | flops 524288 | bytes 2621444 | tf_op jit(solution)/shard_map/scatter-add | solution.py:124
  314.6 2.8 convert_element_type.178
  317.4 1.1 convert_reduce_fusion
  318.5 0.2 fusion.46
  318.8 0.9 multiply_convert_fusion
  319.7 1.0 copy-done.6
  320.6 0.9 slice_bitcast_fusion
  321.6 0.5 all-gather.17.cloned.1.call-update
  322.2 78.1 %reduce-scatter.2.cloned.1.call-done = bf16[32,512]{1,0:T(8,128)(2,1)} async-done(((bf16[1024,512]{1,0:T(8,128)(2,1)}), bf16[32,512]{1,0:T(8,128)(2,1)}) %reduce-scatter.2.cloned.1.call-update) | async-done | bytes 32784 | tf_op jit(solution)/shard_map/reduce_scatter | solution.py:126
  400.2 1.4 convert_element_type.179
  401.6 1.5 collective-permute-start.2
  403.2 6.4 %copy.72 = bf16[4096,512]{0,1:T(8,128)(2,1)} copy(bf16[4096,512]{1,0:T(8,128)(2,1)} %all-gather.15.cloned.1.call-done) | data formatting | bytes 8388608 | tf_op jit(solution)/shard_map/reshape | solution.py:38
  409.6 17.6 %all-gather.17.cloned.1.call-done = bf16[4096,512]{1,0:T(8,128)(2,1)} async-done(((bf16[256,512]{1,0:T(8,128)(2,1)}), bf16[4096,512]{1,0:T(8,128)(2,1)}) %all-gather.17.cloned.1.call-update) | async-done | bytes 4194320 | tf_op jit(solution)/shard_map/all_gather | solution.py:66
  427.2 10.4 %fusion.123 = (f32[256]{0:T(256)S(1)}, f32[4,128,256]{2,1,0:T(8,128)S(1)}) fusion(bf16[4096,4,128]{0,2,1:T(8,128)(2,1)} %bitcast.176, pred[256,4096]{1,0:T(8,128)(4,1)} %get-tuple-element.21, bf16[32,4,8,128]{3,2,1,0:T(8,128)(2,1)} %get-tuple-element.10, bf16[4096,512]{1,0:T(8,128)(2,1)} %all-gather.17.cloned.1.call-done), kind=kOutput, calls=%fused_computation.170 | convolution fusion | flops 2172780288 | bytes 10224640 | tf_op jit(solution)/shard_map/hqk,khd->qhd/dot_general | solution.py:41
  437.7 0.7 copy-done.4
  438.3 1.2 copy.73
  439.6 1.4 fusion.128
  441.0 0.2 multiply_reduce_fusion
  441.2 1.9 fusion.64
  (73 shorter events, 1.9 us)
Async XLA Ops:
  8.0 51.9 %copy-start = (bf16[1,512,2048]{2,1,0:T(8,128)(2,1)S(1)}, bf16[1,512,2048]{2,1,0:T(8,128)(2,1)}, u32[]{:S(2)}) copy-start(bf16[1,512,2048]{2,1,0:T(8,128)(2,1)} %param.13) | copy-start | bytes 6291460
  8.0 34.8 %copy-start.1 = (bf16[1024,512]{1,0:T(8,128)(2,1)S(1)}, bf16[1024,512]{1,0:T(8,128)(2,1)}, u32[]{:S(2)}) copy-start(bf16[1024,512]{1,0:T(8,128)(2,1)} %param.8) | copy-start | bytes 3145732
  8.0 106.9 %all-gather.7.cloned.1.call-start = ((), (), s32[]{:S(2)}) async-start(), calls=%async_computation.4 | async-start | bytes 4456448 | tf_op jit(solution)/shard_map/all_gather | solution.py:67
  59.9 3.6 copy-start.10
  60.8 1.0 copy-start.7
  62.7 105.5 %all-gather.9.cloned.1.call-start = ((), (), s32[]{:S(2)}) async-start(), calls=%async_computation.5 | async-start | bytes 4456448 | tf_op jit(solution)/shard_map/all_gather | solution.py:66
  63.4 175.9 %all-gather.11.cloned.1.call-start = ((), (), s32[]{:S(2)}) async-start(), calls=%async_computation.6 | async-start | bytes 4456448 | tf_op jit(solution)/shard_map/all_gather | solution.py:67
  68.0 115.0 %collective-permute-start = (bf16[256,512]{1,0:T(8,128)(2,1)S(1)}, bf16[256,512]{1,0:T(8,128)(2,1)}, u32[]{:S(2)}, u32[]{:S(2)}) collective-permute-start(bf16[256,512]{1,0:T(8,128)(2,1)S(1)} %gather_fusion.1), channel_id=1, source_target_pairs={{1,0},{3,2},{5,4},{7,6},{9,8},{11,10},{13,12},{15,14},{17,16},{19,... | collective-permute-start | bytes 786440 | tf_op jit(solution)/shard_map/ppermute | solution.py:16
  168.2 11.6 %copy-start.2 = (bf16[1,512,512]{2,1,0:T(8,128)(2,1)S(1)}, bf16[1,512,512]{2,1,0:T(8,128)(2,1)}, u32[]{:S(2)}) copy-start(bf16[1,512,512]{2,1,0:T(8,128)(2,1)} %param.14) | copy-start | bytes 1572868
  181.2 2.7 collective-permute-start.1
  185.3 4.2 copy-start.8
  186.2 1.0 copy-start.5
  188.1 104.4 %all-gather.13.cloned.1.call-start = ((), (), s32[]{:S(2)}) async-start(), calls=%async_computation.7 | async-start | bytes 4456448 | tf_op jit(solution)/shard_map/all_gather | solution.py:66
  223.5 85.5 %all-to-all-start.2 = ((bf16[4,128,512]{2,1,0:T(8,128)(2,1)}), bf16[4,128,512]{2,1,0:T(8,128)(2,1)}, u32[]{:S(2)}, u32[]{:S(2)}) async-start(bf16[4,128,512]{2,1,0:T(8,128)(2,1)} %scatter_fusion.1), calls=%async_computation.2 | async-start | bytes 1048576 | tf_op jit(solution)/shard_map/all_to_all | solution.py:118
  228.1 172.1 %reduce-scatter.2.cloned.1.call-start = ((), (), s32[]{:S(2)}) async-start(), calls=%async_computation.10 | async-start | bytes 1081344 | tf_op jit(solution)/shard_map/reduce_scatter | solution.py:126
  302.8 0.8 copy-start.3
  302.8 3.6 copy-start.9
  307.4 10.0 %collective-permute-start.3 = (bf16[256,512]{1,0:T(8,128)(2,1)S(1)}, bf16[256,512]{1,0:T(8,128)(2,1)S(1)}, u32[]{:S(2)}, u32[]{:S(2)}) collective-permute-start(bf16[256,512]{1,0:T(8,128)(2,1)S(1)} %get-tuple-element.5), channel_id=1, source_target_pairs={{0,1},{2,3},{4,5},{6,7},{8,9},{10,11},{12,13},{14,15},{16,17},{18,... | collective-permute-start | bytes 786440 | tf_op jit(solution)/shard_map/ppermute | solution.py:16
  317.4 85.8 %all-gather.15.cloned.1.call-start = ((), (), s32[]{:S(2)}) async-start(), calls=%async_computation.8 | async-start | bytes 4456448 | tf_op jit(solution)/shard_map/all_gather | solution.py:67
  319.6 1.0 copy-start.6
  321.6 105.6 %all-gather.17.cloned.1.call-start = ((), (), s32[]{:S(2)}) async-start(), calls=%async_computation.9 | async-start | bytes 4456448 | tf_op jit(solution)/shard_map/all_gather | solution.py:66
  401.6 39.6 %collective-permute-start.2 = (bf16[256,512]{1,0:T(8,128)(2,1)}, bf16[256,512]{1,0:T(8,128)(2,1)}, u32[]{:S(2)}, u32[]{:S(2)}) collective-permute-start(bf16[256,512]{1,0:T(8,128)(2,1)} %get-tuple-element.4), channel_id=1, source_target_pairs={{1,0},{3,2},{5,4},{7,6},{9,8},{11,10},{13,12},{15,14},{17,16},{19,... | collective-permute-start | bytes 786440 | tf_op jit(solution)/shard_map/ppermute | solution.py:16
  437.5 0.8 copy-start.4
Sparse Core Ops, SparseCore 0:
  62.8 52.0 all-gather.6
  117.0 51.0 all-gather.8
  188.2 51.0 all-gather.10
  241.3 51.0 all-gather.12
  321.7 52.1 all-gather.14
  375.9 51.2 all-gather.16
Sparse Core Ops, SparseCore 1:
  317.4 82.7 reduce-scatter.1
where the time goes:
time: 453 us; the launch traced here: 450 us
  waiting for transfers between devices  249 us (55%)
  local copies, waits for them, and re-layouts  90.9 us (20%)
  matrix products  38 us (8%)
  other arithmetic  25.6 us (6%)
  blocking collectives  20.2 us (4%)
  between operations  16 us (4%)
  starting transfers between devices  11 us (2%)
    all_gather x3, waiting for transfers between devices, hstu_layer(): lax.all_gather(key_rows, 'row', axis=0, tiled=True)  111 us
    reduce_scatter x1, waiting for transfers between devices, body(): lax.psum_scatter(partial_value.astype(jnp.bfloat16), ('row', 'phase'), sc...  78.1 us
    all_gather x3, waiting for transfers between devices, hstu_layer(): lax.all_gather(value_rows, 'row', axis=0, tiled=True)  56.8 us
    scatter x1, local copies, waits for them, and re-layouts, body(): jnp.zeros((parties, capacity, model_width), jnp.bfloat16).at[owners, places]  34 us
    dot_general x3, matrix products, attend_keys(): jnp.einsum('hqk,khd->qhd', attn_weights, value_heads, preferred_element_t...  31.2 us
    scatter x1, local copies, waits for them, and re-layouts, body(): jnp.full((parties, capacity), -1, jnp.int32).at[owners, places]  21.4 us
    reshape x3, local copies, waits for them, and re-layouts, attend_keys(): value_heads = value_piece.reshape(key_count, HEADS, HEAD_DIM)  19.2 us
    all_to_all x1, blocking collectives, body(): lax.all_to_all(looked, 'emb', split_axis=0, concat_axis=0, tiled=True)  10.7 us
  transfers between devices with their start and end apart: 12, of which 7 were waited for; matrix products, arithmetic and copies ran while one was open for 25% of the time, Pallas kernels for 0%

commit v1 on v0

v1 whole, which is shorter than its diff:
```python
import functools

import jax
import jax.numpy as jnp
from jax import lax
from jax.experimental import pallas as pl
from jax.experimental.pallas import tpu as pltpu
from jax.sharding import PartitionSpec as P

MESH = pl.DeviceIdType.MESH
F32 = jnp.float32
BF16 = jnp.bfloat16
EPS = 1e-05
BIG = 2.0**40

TOK = 256
DIM = 512
HD = 128
CAP = 128
OWNED = 1024

KV_A, Q_A, HOP_R, HOP_L, FAR_K, FAR_V, MIX = 0, 3, 6, 10, 14, 18, 22
PER_SECTION = 25
REQ, ROWS, GRAD, WGT, OWGT, HALF, GA, GB = 50, 53, 56, 59, 60, 61, 62, 65
N_REMOTE = 68


def dot(left, right):
    return jnp.dot(left, right, preferred_element_type=F32)


def layer_norm(values):
    average = jnp.mean(values, axis=-1, keepdims=True)
    centered = values - average
    return centered * lax.rsqrt(jnp.mean(centered * centered, axis=-1, keepdims=True) + EPS)


def silu(v):
    u = 0.5 * v
    return u + u * jnp.tanh(u)


def iota(shape, dim):
    return lax.broadcasted_iota(jnp.int32, shape, dim)


def kernel(
    owner_ref, slot_ref, len_ref, gain_ref, table_hbm, grads_hbm, w_hbm, ow_hbm,
    states_ref, tg_ref,
    table, grads, w_all, ow_all, req_snd, req_rcv, rows_snd, rows_rcv, go_snd, g_rcv,
    x_ref, snd, gates, kv, qs, acc, mix_snd, mix, half_snd, half_own, half_rcv,
    ga_snd, ga_rcv, gb_snd, gb_rcv, ssem, rsem, lsem,
):
    ex = lax.axis_index("emb")
    row = lax.axis_index("row")
    c = lax.axis_index("phase")
    z, y = row // 4, row % 4
    a = z * (1 - c) + y * c
    b = y * (1 - c) + z * c
    sa, sb = 4 - 3 * c, 1 + 3 * c

    def at_a(d):
        return {"row": sa * ((a + d) % 4) + sb * b}

    def at_b(d):
        return {"row": sa * a + sb * ((b + d) % 4)}

    def at_x(d):
        return {"emb": (ex + d) % 4}

    other = {"phase": 1 - c}

    def rc(src, dst, sem, dev):
        return pltpu.make_async_remote_copy(
            src_ref=src, dst_ref=dst, send_sem=ssem.at[sem], recv_sem=rsem.at[sem],
            device_id=dev, device_id_type=MESH,
        )

    cp_table = pltpu.make_async_copy(table_hbm, table, lsem.at[0])
    cp_grads = pltpu.make_async_copy(grads_hbm, grads, lsem.at[1])
    cp_w = pltpu.make_async_copy(w_hbm, w_all.at[c], lsem.at[2])
    cp_ow = pltpu.make_async_copy(ow_hbm, ow_all.at[c], lsem.at[3])
    for cp in (cp_table, cp_grads, cp_w, cp_ow):
        cp.start()
    barrier = pltpu.get_barrier_semaphore()
    for d in (1, 2, 3):
        for dev in (at_x(d), at_a(d), at_b(d)):
            pl.semaphore_signal(barrier, inc=1, device_id=dev, device_id_type=MESH)
    pl.semaphore_signal(barrier, inc=1, device_id=other, device_id_type=MESH)

    own_row = owner_ref[...].astype(F32)
    slot_row = slot_ref[...].astype(F32)
    ti, tj = iota((TOK, TOK), 0), iota((TOK, TOK), 1)
    eye = ti == tj
    own_col = jnp.sum(jnp.where(eye, own_row, 0.0), axis=1, keepdims=True)
    slot_col = jnp.sum(jnp.where(eye, slot_row, 0.0), axis=1, keepdims=True)
    same = own_col == own_row
    rank_col = jnp.sum(jnp.where(same & (tj < ti), 1.0, 0.0), axis=1, keepdims=True)
    rank_row = jnp.sum(jnp.where(same & (ti < tj), 1.0, 0.0), axis=0, keepdims=True)
    key_col = (own_col * CAP + rank_col).astype(jnp.int32)
    key_row = (own_row * CAP + rank_row).astype(jnp.int32)
    place = key_col == iota((TOK, 4 * CAP), 1)
    req_row = jnp.sum(jnp.where(place, slot_col + 1.0, 0.0), axis=0, keepdims=True) - 1.0
    for e in range(4):
        req_snd[e] = jnp.broadcast_to(req_row[:, e * CAP : (e + 1) * CAP], (8, CAP))
    cp_req = pltpu.make_async_copy(req_snd.at[ex], req_rcv.at[ex], lsem.at[4])
    cp_req.start()
    pl.semaphore_wait(barrier, 10)
    req = [rc(req_snd.at[(ex + d) % 4], req_rcv.at[ex], REQ + d - 1, at_x(d)) for d in (1, 2, 3)]
    for d in (2, 1, 3):
        req[d - 1].start()
    wgt = rc(w_hbm, w_all.at[c], WGT, other)
    owgt = rc(ow_hbm, ow_all.at[c], OWGT, other)
    wgt.start()
    owgt.start()

    cp_grads.wait()
    place_t = (key_row == iota((4 * CAP, TOK), 0)).astype(F32).astype(BF16)
    for e in range(4):
        go_snd[e] = dot(place_t[e * CAP : (e + 1) * CAP], grads[...]).astype(BF16)
    cp_go = pltpu.make_async_copy(go_snd.at[ex], g_rcv.at[ex], lsem.at[5])
    cp_go.start()

    cp_req.wait()
    cp_table.wait()
    eye_cap = iota((CAP, CAP), 0) == iota((CAP, CAP), 1)

    def look_up(q):
        wanted = jnp.sum(
            jnp.where(eye_cap, req_rcv[q][0:1], 0.0), axis=1, keepdims=True
        ).astype(jnp.int32)
        picked = (wanted == iota((CAP, OWNED), 1)).astype(F32).astype(BF16)
        rows_snd[q] = dot(picked, table[...]).astype(BF16)

    rows = [rc(rows_snd.at[(ex + d) % 4], rows_rcv.at[ex], ROWS + d - 1, at_x(d)) for d in (1, 2, 3)]
    for d in (3, 1, 2):
        req[d - 1].wait_recv()
        look_up((ex + 4 - d) % 4)
        rows[3 - d].start()
    look_up(ex)
    cp_rows = pltpu.make_async_copy(rows_snd.at[ex], rows_rcv.at[ex], lsem.at[6])
    cp_rows.start()
    cp_rows.wait()
    for d in (1, 2, 3):
        rows[d - 1].wait_recv()
    embedded = dot(
        place.astype(F32).astype(BF16), rows_rcv[...].reshape(4 * CAP, DIM)
    )
    x_ref[...] = embedded.astype(BF16)

    grad = [rc(go_snd.at[(ex + d) % 4], g_rcv.at[ex], GRAD + d - 1, at_x(d)) for d in (1, 2, 3)]
    for d in (2, 1, 3):
        grad[d - 1].start()
    cp_w.wait()
    cp_ow.wait()
    wgt.wait_recv()
    owgt.wait_recv()

    bound = len_ref[c, 0]
    lane0 = iota((TOK, HD), 1) == 0
    pos = iota((TOK, HD), 0)
    diff = ti - tj

    def partial_half(cc):
        j = iota((512, 1), 0)
        aj, bj, i = j // 128, (j // 32) % 4, j % 32
        slot = ((4 - 3 * cc) * aj + (1 + 3 * cc) * bj) * 64 + cc * 32 + i
        total = None
        for q in range(4):
            hit = (slot == req_rcv[q][0:1].astype(jnp.int32)).astype(F32).astype(BF16)
            term = dot(hit, g_rcv[q])
            total = term if total is None else total + term
        return total

    half = rc(half_snd, half_rcv, HALF, other)
    ga = [rc(ga_snd.at[(a + d) % 4], ga_rcv.at[a], GA + d - 1, at_a(d)) for d in (1, 2, 3)]
    gb = [rc(gb_snd.at[(b + d) % 4], gb_rcv.at[b], GB + d - 1, at_b(d)) for d in (1, 2, 3)]

    for s in (0, 1):
        base = s * PER_SECTION
        normed = layer_norm(x_ref[...].astype(F32)).astype(BF16)
        kv_a = [rc(snd.at[(a + d) % 4, pl.ds(0, 2)], kv.at[s, b, a], base + KV_A + d - 1, at_a(d)) for d in (1, 2, 3)]
        q_a = [rc(snd.at[(a + d) % 4, 2], qs.at[s, a], base + Q_A + d - 1, at_a(d)) for d in (1, 2, 3)]
        mixs = [rc(mix_snd.at[(a + d) % 4], mix.at[s, a], base + MIX + d - 1, at_a(d)) for d in (1, 2, 3)]

        def hop_r(i, base=base, s=s):
            block = kv.at[s, b, (a + 4 - i) % 4]
            return rc(block, block, base + HOP_R + i, at_b(1))

        def hop_l(i, base=base, s=s):
            block = kv.at[s, b, (a + 4 - i) % 4]
            return rc(block, block, base + HOP_L + i, at_b(3))

        def far_k(i, base=base, s=s):
            block = kv.at[s, (b + 3) % 4, (a + 4 - i) % 4, 0]
            return rc(block, block, base + FAR_K + i, at_b(1))

        def far_v(i, base=base, s=s):
            block = kv.at[s, (b + 1) % 4, (a + 4 - i) % 4, 1]
            return rc(block, block, base + FAR_V + i, at_b(3))

        def project(part, column, scale):
            made = silu(dot(normed, w_all[s, :, column : column + DIM])) * scale
            for h in range(4):
                snd[h, part] = made[:, h * HD : (h + 1) * HD].astype(BF16)

        project(0, 1536, 1.0)
        project(1, 512, 1.0)
        for d in (2, 1, 3):
            kv_a[d - 1].start()
        cp_kv = pltpu.make_async_copy(snd.at[a, pl.ds(0, 2)], kv.at[s, b, a], lsem.at[7])
        cp_kv.start()
        cp_kv.wait()
        hop_r(0).start()
        hop_l(0).start()
        project(2, 1024, 0.5)
        for d in (2, 1, 3):
            q_a[d - 1].start()
        cp_q = pltpu.make_async_copy(snd.at[a, 2], qs.at[s, a], lsem.at[8])
        cp_q.start()
        for d in (1, 2, 3):
            kv_a[d - 1].wait_recv()
            hop_r(d).start()
            hop_l(d).start()
        gates[...] = silu(dot(normed, w_all[s, :, 0:DIM])).astype(BF16)
        acc[...] = jnp.zeros_like(acc)
        if s == 1:
            half.wait_recv()
            summed = half_own[...] + half_rcv[...].astype(F32)
            half_own[...] = summed
            for k in range(4):
                ga_snd[k] = summed[k * 128 : (k + 1) * 128].astype(BF16)
            for d in (2, 1, 3):
                ga[d - 1].start()
        cp_q.wait()
        for d in (1, 2, 3):
            q_a[d - 1].wait_recv()

        def attend(bb, aa, s=s):
            key_row0 = 256 * (sa * aa + sb * bb)
            before = (pos + key_row0 < bound) & lane0
            keys = jnp.concatenate(
                [kv[s, bb, aa, 0], jnp.where(before, 1.0, 0.0).astype(BF16)], axis=1
            )
            values = kv[s, bb, aa, 1]
            for k in range(4):
                query_row0 = 256 * (sa * k + sb * b)
                after = (pos + query_row0 >= bound) & lane0
                queries = jnp.concatenate(
                    [qs[s, k], jnp.where(after, -BIG, 0.0).astype(BF16)], axis=1
                )
                u = lax.dot_general(
                    queries, keys, (((1,), (1,)), ((), ())), preferred_element_type=F32
                )
                weights = jnp.where(diff >= key_row0 - query_row0, u + u * jnp.tanh(u), 0.0)
                acc[k] += dot(weights.astype(BF16), values)

        def step(n, carry):
            stage, i = n // 4, n % 4

            @pl.when(stage == 0)
            def _():
                hop_r(i).wait_recv()
                far_k(i).start()
                hop_l(i).wait_recv()
                far_v(i).start()

            @pl.when(stage == 3)
            def _():
                far_k(i).wait_recv()
                far_v(i).wait_recv()

            turn = 3 * (stage % 2) + (stage // 2) * (1 - stage % 2) - (stage // 3)
            bb = (b + turn) % 4

            @pl.when((c == 0) | (bb <= b))
            def _():
                attend(bb, (a + 4 - i) % 4)

            return carry

        lax.fori_loop(0, 16, step, 0)
        for k in range(4):
            mix_snd[k] = acc[k].astype(BF16)
        for d in (2, 1, 3):
            mixs[d - 1].start()
        cp_mix = pltpu.make_async_copy(mix_snd.at[a], mix.at[s, a], lsem.at[9])
        cp_mix.start()

        if s == 0:
            cp_go.wait()
            for d in (1, 2, 3):
                grad[d - 1].wait_recv()
            half_snd[...] = partial_half(1 - c).astype(BF16)
            half.start()
            half_own[...] = partial_half(c)
        else:
            for d in (1, 2, 3):
                ga[d - 1].wait_recv()
            total = half_own[pl.ds(pl.multiple_of(a * 128, 128), 128), :]
            for d in (1, 2, 3):
                total = total + ga_rcv[(a + d) % 4].astype(F32)
            half_own[0:128, :] = total
            for k in range(4):
                gb_snd[k] = total[k * 32 : (k + 1) * 32].astype(BF16)
            for d in (2, 1, 3):
                gb[d - 1].start()

        cp_mix.wait()
        for d in (1, 2, 3):
            mixs[d - 1].wait_recv()
        mixed = jnp.concatenate([mix[s, h] for h in range(4)], axis=1).astype(F32)
        gated = (layer_norm(mixed) * gates[...].astype(F32)).astype(BF16)
        residual = x_ref[...].astype(F32) + dot(gated, ow_all[s])
        if s == 0:
            x_ref[...] = residual.astype(BF16)
        else:
            states_ref[...] = (layer_norm(residual) * gain_ref[...]).astype(BF16)
        for d in (1, 2, 3):
            kv_a[d - 1].wait_send()
            q_a[d - 1].wait_send()
            mixs[d - 1].wait_send()

        def drain(i, carry):
            hop_r(i).wait_send()
            hop_l(i).wait_send()
            far_k(i).wait_send()
            far_v(i).wait_send()
            return carry

        lax.fori_loop(0, 4, drain, 0)

    for d in (1, 2, 3):
        gb[d - 1].wait_recv()
    total = half_own[pl.ds(pl.multiple_of(b * 32, 32), 32), :]
    for d in (1, 2, 3):
        total = total + gb_rcv[(b + d) % 4].astype(F32)
    tg_ref[...] = total
    for cp in req + rows + grad + [wgt, owgt, half] + ga + gb:
        cp.wait_send()


def body(
    item_table, item_owner, item_slot, seq_lengths, row_grads, proj_weight, out_weight, final_gain
):
    vmem = pl.BlockSpec(memory_space=pltpu.VMEM)
    hbm = pl.BlockSpec(memory_space=pl.ANY)
    smem = pl.BlockSpec(memory_space=pltpu.SMEM)

    def buf(*shape, dtype=BF16):
        return pltpu.VMEM(shape, dtype)

    states, table_grad = pl.pallas_call(
        kernel,
        out_shape=(
            jax.ShapeDtypeStruct((TOK, DIM), BF16),
            jax.ShapeDtypeStruct((32, DIM), F32),
        ),
        in_specs=[vmem, vmem, smem, vmem, hbm, hbm, hbm, hbm],
        out_specs=(vmem, vmem),
        scratch_shapes=[
            buf(OWNED, DIM), buf(TOK, DIM), buf(2, DIM, 4 * DIM), buf(2, DIM, DIM),
            buf(4, 8, CAP, dtype=F32), buf(4, 8, CAP, dtype=F32),
            buf(4, CAP, DIM), buf(4, CAP, DIM), buf(4, CAP, DIM), buf(4, CAP, DIM),
            buf(TOK, DIM), buf(4, 3, TOK, HD), buf(TOK, DIM),
            buf(2, 4, 4, 2, TOK, HD), buf(2, 4, TOK, HD), buf(4, TOK, HD, dtype=F32),
            buf(4, TOK, HD), buf(2, 4, TOK, HD),
            buf(512, DIM), buf(512, DIM, dtype=F32), buf(512, DIM),
            buf(4, 128, DIM), buf(4, 128, DIM), buf(4, 32, DIM), buf(4, 32, DIM),
            pltpu.SemaphoreType.DMA((N_REMOTE,)),
            pltpu.SemaphoreType.DMA((N_REMOTE,)),
            pltpu.SemaphoreType.DMA((10,)),
        ],
        compiler_params=pltpu.CompilerParams(
            collective_id=0, has_side_effects=True, vmem_limit_bytes=56 << 20
        ),
    )(
        item_owner.reshape(1, TOK),
        item_slot.reshape(1, TOK),
        seq_lengths.reshape(2, 2),
        final_gain.reshape(1, DIM),
        item_table,
        row_grads.reshape(TOK, DIM),
        proj_weight.reshape(DIM, 4 * DIM),
        out_weight.reshape(DIM, DIM),
    )
    return states.reshape(1, 1, TOK, DIM), table_grad


def solution(mesh):
    placed = (
        P("emb", None),
        P("emb", "phase", "row", None),
        P("emb", "phase", "row"),
        P("emb", None, None),
        P("emb", "phase", "row", None),
        P("phase", None, None),
        P("phase", None, None),
        P(),
    )
    return jax.shard_map(
        body,
        mesh=mesh,
        in_specs=placed,
        out_specs=(P("emb", "phase", "row", None), P(("emb", "row", "phase"), None)),
        check_vma=False,
    )
```

time: 453 us -> 87.1 us (0.19)
  waiting for transfers between devices: 249 us -> 0 us
  local copies, waits for them, and re-layouts: 90.9 us -> 3.14 us
  Pallas kernels: 0 us -> 83.1 us
  matrix products: 38 us -> 0 us
  other arithmetic: 25.6 us -> 0 us
  blocking collectives: 20.2 us -> 0 us
  between operations: 16 us -> 0.64 us
  starting transfers between devices: 11 us -> 0 us
    all_gather x6 -> x0, waiting for transfers between devices: 168 us -> none  [the longest x3 111 us: hstu_layer(): lax.all_gather(key_rows, 'row', axis=0, tiled=True)]
    pallas_call x0 -> x1, Pallas kernels: none -> 83.1 us  [body(): pl.pallas_call(kernel, out_shape=(jax.ShapeDtypeStruct((TOK, DIM), BF16),...]
    reduce_scatter x1 -> x0, waiting for transfers between devices: 78.1 us -> none  [body(): lax.psum_scatter(partial_value.astype(jnp.bfloat16), ('row', 'phase'), sc...]
    scatter x2 -> x0, local copies, waits for them, and re-layouts: 55.3 us -> none  [the longest x1 34 us: body(): jnp.zeros((parties, capacity, model_width), jnp.bfloat16).at[owners, places]]
    dot_general x9 -> x0, matrix products: 38 us -> none  [the longest x3 31.2 us: attend_keys(): jnp.einsum('hqk,khd->qhd', attn_weights, value_heads, preferred_element_t...]
    reshape x6 -> x0, local copies, waits for them, and re-layouts: 22.7 us -> none  [the longest x3 19.2 us: attend_keys(): value_heads = value_piece.reshape(key_count, HEADS, HEAD_DIM)]
    all_to_all x2 -> x0, blocking collectives: 20.2 us -> none  [the longest x1 10.7 us: body(): lax.all_to_all(looked, 'emb', split_axis=0, concat_axis=0, tiled=True)]
    ppermute x4 -> x0, starting transfers between devices: 6.12 us -> none  [passed_along(): return lax.ppermute(shard, axis, pairs)]
  transfers between devices with their start and end apart: 12 -> 0, of which waited for: 7 -> 0; matrix products, arithmetic and copies ran while one was open for 25% -> 0% of each run, Pallas kernels for 0% -> 0%
where the time goes in v1:
time: 87.1 us; the launch traced here: 86.8 us
  Pallas kernels  83.1 us (95%)
  local copies, waits for them, and re-layouts  3.14 us (4%)
    pallas_call x1, Pallas kernels, body(): pl.pallas_call(kernel, out_shape=(jax.ShapeDtypeStruct((TOK, DIM), BF16),...  83.1 us
    unnamed x2, local copies, waits for them, and re-layouts  3.14 us

profile of v1, /device:TPU:0, one launch (start us, length us, event | category | flops | bytes accessed | tf_op | source)
XLA Modules:
  0.0 86.8 jit_solution(6343873893104216543)
XLA Ops:
  0.6 83.1 %shard_map.95 = (bf16[256,512]{1,0:T(8,128)(2,1)}, f32[32,512]{1,0:T(8,128)}) custom-call(s32[1,256]{1,0:T(1,128)} %bitcast.13, s32[1,256]{1,0:T(1,128)} %bitcast.14, s32[2,2]{1,0:T(2,128)} %bitcast.15, f32[1,512]{1,0:T(1,128)} %bitcast.12, bf16[1024,512]{1,0:T(8,128)(2,1)} %table_hbm.1, bf16[256,512]{1,0:T(8,128)(2,1)} %bitcast.10, ...), custom_call_target="tpu_custom_call" | custom-call | tf_op jit(solution)/shard_map/pallas_call | solution.py:353
  83.7 1.7 %copy.12 = bf16[1,1,256,512]{3,2,1,0:T(8,128)(2,1)} copy(bf16[1,1,256,512]{3,2,1,0:T(8,128)(2,1)} %bitcast.11) | data formatting | bytes 524288
  85.4 1.5 %copy.13 = f32[32,512]{1,0:T(8,128)} copy(f32[32,512]{1,0:T(8,128)} %get-tuple-element.9) | data formatting | bytes 131072

commit v2 on v1

--- a/solution.py
+++ b/solution.py
@@ -49,7 +49,7 @@
     states_ref, tg_ref,
     table, grads, w_all, ow_all, req_snd, req_rcv, rows_snd, rows_rcv, go_snd, g_rcv,
     x_ref, snd, gates, kv, qs, acc, mix_snd, mix, half_snd, half_own, half_rcv,
-    ga_snd, ga_rcv, gb_snd, gb_rcv, ssem, rsem, lsem,
+    ga_snd, ga_rcv, gb_snd, gb_rcv, q_ext, k_ext, diff_ref, ssem, rsem, lsem,
 ):
     ex = lax.axis_index("emb")
     row = lax.axis_index("row")
@@ -105,6 +105,16 @@
         req_snd[e] = jnp.broadcast_to(req_row[:, e * CAP : (e + 1) * CAP], (8, CAP))
     cp_req = pltpu.make_async_copy(req_snd.at[ex], req_rcv.at[ex], lsem.at[4])
     cp_req.start()
+    bound = len_ref[c, 0]
+    lane0 = iota((TOK, HD), 1) == 0
+    pos = iota((TOK, HD), 0)
+    diff_ref[...] = ti - tj
+    for k in range(4):
+        after = (pos + 256 * (sa * k + sb * b) >= bound) & lane0
+        q_ext[k] = jnp.where(after, -BIG, 0.0).astype(BF16)
+        for h in range(4):
+            before = (pos + 256 * (sa * k + sb * h) < bound) & lane0
+            k_ext[h, k] = jnp.where(before, 1.0, 0.0).astype(BF16)
     pl.semaphore_wait(barrier, 10)
     req = [rc(req_snd.at[(ex + d) % 4], req_rcv.at[ex], REQ + d - 1, at_x(d)) for d in (1, 2, 3)]
     for d in (2, 1, 3):
@@ -133,13 +143,13 @@
         rows_snd[q] = dot(picked, table[...]).astype(BF16)
 
     rows = [rc(rows_snd.at[(ex + d) % 4], rows_rcv.at[ex], ROWS + d - 1, at_x(d)) for d in (1, 2, 3)]
-    for d in (3, 1, 2):
+    look_up(ex)
+    cp_rows = pltpu.make_async_copy(rows_snd.at[ex], rows_rcv.at[ex], lsem.at[6])
+    cp_rows.start()
+    for d in (1, 3, 2):
         req[d - 1].wait_recv()
         look_up((ex + 4 - d) % 4)
         rows[3 - d].start()
-    look_up(ex)
-    cp_rows = pltpu.make_async_copy(rows_snd.at[ex], rows_rcv.at[ex], lsem.at[6])
-    cp_rows.start()
     cp_rows.wait()
     for d in (1, 2, 3):
         rows[d - 1].wait_recv()
@@ -155,11 +165,6 @@
     cp_ow.wait()
     wgt.wait_recv()
     owgt.wait_recv()
-
-    bound = len_ref[c, 0]
-    lane0 = iota((TOK, HD), 1) == 0
-    pos = iota((TOK, HD), 0)
-    diff = ti - tj
 
     def partial_half(cc):
         j = iota((512, 1), 0)
@@ -176,159 +181,300 @@
     ga = [rc(ga_snd.at[(a + d) % 4], ga_rcv.at[a], GA + d - 1, at_a(d)) for d in (1, 2, 3)]
     gb = [rc(gb_snd.at[(b + d) % 4], gb_rcv.at[b], GB + d - 1, at_b(d)) for d in (1, 2, 3)]
 
-    for s in (0, 1):
-        base = s * PER_SECTION
+    def kv_a(s, d):
+        return rc(snd.at[s, (a + d) % 4, pl.ds(0, 2)], kv.at[s, b, a], s * PER_SECTION + KV_A + d - 1, at_a(d))
+
+    def q_a(s, d):
+        return rc(snd.at[s, (a + d) % 4, 2], qs.at[s, a], s * PER_SECTION + Q_A + d - 1, at_a(d))
+
+    def mix_a(s, d):
+        return rc(mix_snd.at[s, (a + d) % 4], mix.at[s, a], s * PER_SECTION + MIX + d - 1, at_a(d))
+
+    def hop_r(s, r):
+        block = kv.at[s, b, r]
+        return rc(block, block, s * PER_SECTION + HOP_R + r, at_b(1))
+
+    def hop_l(s, r):
+        block = kv.at[s, b, r]
+        return rc(block, block, s * PER_SECTION + HOP_L + r, at_b(3))
+
+    def hop_v(s, r):
+        block = kv.at[s, b, r, 1]
+        return rc(block, block, s * PER_SECTION + HOP_L + r, at_b(3))
+
+    def far_k(s, r):
+        block = kv.at[s, (b + 3) % 4, r, 0]
+        return rc(block, block, s * PER_SECTION + FAR_K + r, at_b(1))
+
+    def far_kv(s, r):
+        block = kv.at[s, (b + 3) % 4, r]
+        return rc(block, block, s * PER_SECTION + FAR_K + r, at_b(1))
+
+    def far_v(s, r):
+        block = kv.at[s, (b + 1) % 4, r, 1]
+        return rc(block, block, s * PER_SECTION + FAR_V + r, at_b(3))
+
+    uses_l = (c == 0) | (b > 0)
+    uses_r = (c == 0) | (b == 3)
+    sends_r = (c == 0) | (b < 3)
+    sends_l = (c == 0) | (b == 0)
+    sends_v = (c == 1) & (b == 1)
+    sends_far_k = (c == 0) | (b == 2)
+    sends_far_kv = (c == 1) & (b == 1)
+    sends_far_v = (c == 0) | (b == 0)
+
+    def start_hops(s, r):
+        @pl.when(sends_r)
+        def _():
+            hop_r(s, r).start()
+
+        @pl.when(sends_l)
+        def _():
+            hop_l(s, r).start()
+
+        @pl.when(sends_v)
+        def _():
+            hop_v(s, r).start()
+
+    def take_left(s, r):
+        @pl.when(uses_l)
+        def _():
+            hop_r(s, r).wait_recv()
+
+        @pl.when(sends_far_k)
+        def _():
+            far_k(s, r).start()
+
+        @pl.when(sends_far_kv)
+        def _():
+            far_kv(s, r).start()
+
+    def take_right(s, r):
+        @pl.when(uses_r)
+        def _():
+            hop_l(s, r).wait_recv()
+
+        @pl.when((c == 1) & (b == 0))
+        def _():
+            hop_v(s, r).wait_recv()
+
+        @pl.when(sends_far_v)
+        def _():
+            far_v(s, r).start()
+
+    def take_far(s, r):
+        @pl.when(uses_r)
+        def _():
+            far_k(s, r).wait_recv()
+            far_v(s, r).wait_recv()
+
+        @pl.when((c == 1) & (b == 2))
+        def _():
+            far_kv(s, r).wait_recv()
+
+    def section_start(s):
         normed = layer_norm(x_ref[...].astype(F32)).astype(BF16)
-        kv_a = [rc(snd.at[(a + d) % 4, pl.ds(0, 2)], kv.at[s, b, a], base + KV_A + d - 1, at_a(d)) for d in (1, 2, 3)]
-        q_a = [rc(snd.at[(a + d) % 4, 2], qs.at[s, a], base + Q_A + d - 1, at_a(d)) for d in (1, 2, 3)]
-        mixs = [rc(mix_snd.at[(a + d) % 4], mix.at[s, a], base + MIX + d - 1, at_a(d)) for d in (1, 2, 3)]
-
-        def hop_r(i, base=base, s=s):
-            block = kv.at[s, b, (a + 4 - i) % 4]
-            return rc(block, block, base + HOP_R + i, at_b(1))
-
-        def hop_l(i, base=base, s=s):
-            block = kv.at[s, b, (a + 4 - i) % 4]
-            return rc(block, block, base + HOP_L + i, at_b(3))
-
-        def far_k(i, base=base, s=s):
-            block = kv.at[s, (b + 3) % 4, (a + 4 - i) % 4, 0]
-            return rc(block, block, base + FAR_K + i, at_b(1))
-
-        def far_v(i, base=base, s=s):
-            block = kv.at[s, (b + 1) % 4, (a + 4 - i) % 4, 1]
-            return rc(block, block, base + FAR_V + i, at_b(3))
 
         def project(part, column, scale):
             made = silu(dot(normed, w_all[s, :, column : column + DIM])) * scale
             for h in range(4):
-                snd[h, part] = made[:, h * HD : (h + 1) * HD].astype(BF16)
+                snd[s, h, part] = made[:, h * HD : (h + 1) * HD].astype(BF16)
 
         project(0, 1536, 1.0)
         project(1, 512, 1.0)
-        for d in (2, 1, 3):
-            kv_a[d - 1].start()
-        cp_kv = pltpu.make_async_copy(snd.at[a, pl.ds(0, 2)], kv.at[s, b, a], lsem.at[7])
+        for d in (1, 3):
+            kv_a(s, d).start()
+        cp_kv = pltpu.make_async_copy(snd.at[s, a, pl.ds(0, 2)], kv.at[s, b, a], lsem.at[7])
         cp_kv.start()
         cp_kv.wait()
-        hop_r(0).start()
-        hop_l(0).start()
+
+        @pl.when(c == 0)
+        def _():
+            start_hops(s, a)
+
         project(2, 1024, 0.5)
-        for d in (2, 1, 3):
-            q_a[d - 1].start()
-        cp_q = pltpu.make_async_copy(snd.at[a, 2], qs.at[s, a], lsem.at[8])
+        cp_q = pltpu.make_async_copy(snd.at[s, a, 2], qs.at[s, a], lsem.at[8])
         cp_q.start()
+        gates[...] = silu(dot(normed, w_all[s, :, 0:DIM])).astype(BF16)
+        cp_q.wait()
+        kv_a(s, 1).wait_send()
+        kv_a(s, 3).wait_send()
+        kv_a(s, 2).start()
+        for d in (1, 3, 2):
+            q_a(s, d).start()
+
+    def section_end(s):
         for d in (1, 2, 3):
-            kv_a[d - 1].wait_recv()
-            hop_r(d).start()
-            hop_l(d).start()
-        gates[...] = silu(dot(normed, w_all[s, :, 0:DIM])).astype(BF16)
-        acc[...] = jnp.zeros_like(acc)
-        if s == 1:
-            half.wait_recv()
-            summed = half_own[...] + half_rcv[...].astype(F32)
-            half_own[...] = summed
-            for k in range(4):
-                ga_snd[k] = summed[k * 128 : (k + 1) * 128].astype(BF16)
-            for d in (2, 1, 3):
-                ga[d - 1].start()
-        cp_q.wait()
-        for d in (1, 2, 3):
-            q_a[d - 1].wait_recv()
-
-        def attend(bb, aa, s=s):
-            key_row0 = 256 * (sa * aa + sb * bb)
-            before = (pos + key_row0 < bound) & lane0
-            keys = jnp.concatenate(
-                [kv[s, bb, aa, 0], jnp.where(before, 1.0, 0.0).astype(BF16)], axis=1
-            )
-            values = kv[s, bb, aa, 1]
-            for k in range(4):
-                query_row0 = 256 * (sa * k + sb * b)
-                after = (pos + query_row0 >= bound) & lane0
-                queries = jnp.concatenate(
-                    [qs[s, k], jnp.where(after, -BIG, 0.0).astype(BF16)], axis=1
-                )
-                u = lax.dot_general(
-                    queries, keys, (((1,), (1,)), ((), ())), preferred_element_type=F32
-                )
-                weights = jnp.where(diff >= key_row0 - query_row0, u + u * jnp.tanh(u), 0.0)
-                acc[k] += dot(weights.astype(BF16), values)
-
-        def step(n, carry):
-            stage, i = n // 4, n % 4
-
-            @pl.when(stage == 0)
-            def _():
-                hop_r(i).wait_recv()
-                far_k(i).start()
-                hop_l(i).wait_recv()
-                far_v(i).start()
-
-            @pl.when(stage == 3)
-            def _():
-                far_k(i).wait_recv()
-                far_v(i).wait_recv()
-
-            turn = 3 * (stage % 2) + (stage // 2) * (1 - stage % 2) - (stage // 3)
-            bb = (b + turn) % 4
-
-            @pl.when((c == 0) | (bb <= b))
-            def _():
-                attend(bb, (a + 4 - i) % 4)
-
-            return carry
-
-        lax.fori_loop(0, 16, step, 0)
-        for k in range(4):
-            mix_snd[k] = acc[k].astype(BF16)
-        for d in (2, 1, 3):
-            mixs[d - 1].start()
-        cp_mix = pltpu.make_async_copy(mix_snd.at[a], mix.at[s, a], lsem.at[9])
-        cp_mix.start()
-
-        if s == 0:
-            cp_go.wait()
-            for d in (1, 2, 3):
-                grad[d - 1].wait_recv()
-            half_snd[...] = partial_half(1 - c).astype(BF16)
-            half.start()
-            half_own[...] = partial_half(c)
-        else:
-            for d in (1, 2, 3):
-                ga[d - 1].wait_recv()
-            total = half_own[pl.ds(pl.multiple_of(a * 128, 128), 128), :]
-            for d in (1, 2, 3):
-                total = total + ga_rcv[(a + d) % 4].astype(F32)
-            half_own[0:128, :] = total
-            for k in range(4):
-                gb_snd[k] = total[k * 32 : (k + 1) * 32].astype(BF16)
-            for d in (2, 1, 3):
-                gb[d - 1].start()
-
-        cp_mix.wait()
-        for d in (1, 2, 3):
-            mixs[d - 1].wait_recv()
+            mix_a(s, d).wait_recv()
         mixed = jnp.concatenate([mix[s, h] for h in range(4)], axis=1).astype(F32)
         gated = (layer_norm(mixed) * gates[...].astype(F32)).astype(BF16)
-        residual = x_ref[...].astype(F32) + dot(gated, ow_all[s])
-        if s == 0:
-            x_ref[...] = residual.astype(BF16)
-        else:
-            states_ref[...] = (layer_norm(residual) * gain_ref[...]).astype(BF16)
+        return x_ref[...].astype(F32) + dot(gated, ow_all[s])
+
+    def send_mix(s, r):
+        @pl.when(r == a)
+        def _():
+            mix[s, a] = acc[r].astype(BF16)
+
+        @pl.when(r != a)
+        def _():
+            mix_snd[s, r] = acc[r].astype(BF16)
+            mix_a(s, (r + 4 - a) % 4).start()
+
+    def attend(s, bb, rows, firsts):
+        terms = []
+        for r, first in zip(rows, firsts):
+            keys = jnp.concatenate([kv[s, bb, r, 0], k_ext[bb, r]], axis=1)
+            m = (4 - first) * TOK
+            queries = jnp.concatenate(
+                [qs[s, first:4].reshape(m, HD), q_ext[first:4].reshape(m, HD)], axis=1
+            )
+            u = lax.dot_general(
+                queries, keys, (((1,), (1,)), ((), ())), preferred_element_type=F32
+            )
+            weights = u + u * jnp.tanh(u)
+            ahead = 256 * (sa * r + sb * bb) - 256 * (sa * first + sb * b)
+            head = jnp.where(diff_ref[...] >= ahead, weights[:TOK], 0.0)
+            weights = jnp.concatenate([head, weights[TOK:]], axis=0) if first < 3 else head
+            terms.append(dot(weights.astype(BF16), kv[s, bb, r, 1]))
+        low, high = firsts
+        apart = (high - low) * TOK
+        if apart:
+            acc[low:high] += terms[0][:apart].reshape(high - low, TOK, HD)
+        acc[high:4] += (terms[0][apart:] + terms[1]).reshape(4 - high, TOK, HD)
+
+    def grad_partials():
         for d in (1, 2, 3):
-            kv_a[d - 1].wait_send()
-            q_a[d - 1].wait_send()
-            mixs[d - 1].wait_send()
-
-        def drain(i, carry):
-            hop_r(i).wait_send()
-            hop_l(i).wait_send()
-            far_k(i).wait_send()
-            far_v(i).wait_send()
+            grad[d - 1].wait_recv()
+        half_snd[...] = partial_half(1 - c).astype(BF16)
+        half.start()
+        half_own[...] = partial_half(c)
+
+    def grad_stage_a():
+        half.wait_recv()
+        summed = half_own[...] + half_rcv[...].astype(F32)
+        half_own[...] = summed
+        for k in range(4):
+            ga_snd[k] = summed[k * 128 : (k + 1) * 128].astype(BF16)
+        for d in (2, 1, 3):
+            ga[d - 1].start()
+
+    def grad_stage_b():
+        for d in (1, 2, 3):
+            ga[d - 1].wait_recv()
+        total = half_own[pl.ds(pl.multiple_of(a * 128, 128), 128), :]
+        for d in (1, 2, 3):
+            total = total + ga_rcv[(a + d) % 4].astype(F32)
+        half_own[0:128, :] = total
+        for k in range(4):
+            gb_snd[k] = total[k * 32 : (k + 1) * 32].astype(BF16)
+        for d in (2, 1, 3):
+            gb[d - 1].start()
+
+    def section(s, carry):
+        @pl.when(s == 1)
+        def _():
+            x_ref[...] = section_end(0).astype(BF16)
+
+        section_start(s)
+        acc[...] = jnp.zeros_like(acc)
+        for d in (1, 3, 2):
+            kv_a(s, d).wait_recv()
+
+            @pl.when(c == 0)
+            def _(d=d):
+                start_hops(s, (a + 4 - d) % 4)
+
+        @pl.when(c == 1)
+        def _():
+            for d in (0, 1, 3, 2):
+                start_hops(s, (a + 4 - d) % 4)
+
+        for d in (1, 3, 2):
+            q_a(s, d).wait_recv()
+
+        take_left(s, a)
+        take_right(s, a)
+
+        def take_pair(take, p):
+            for k in (0, 1):
+
+                @pl.when(2 * p + k != a)
+                def _(k=k):
+                    take(s, 2 * p + k)
+
+        def step(n, carry):
+            own, far = n < 2, n >= 6
+            side = n % 2
+            p = jnp.where(own, n, jnp.where(far, n - 6, (n - 2) // 2))
+            bb = (b + jnp.where(own, 0, jnp.where(far, 2, 3 - 2 * side))) % 4
+            near = (n >= 2) & (n < 6)
+
+            @pl.when(near & (side == 0))
+            def _():
+                take_pair(take_left, p)
+                take_pair(take_right, p)
+
+            @pl.when((s == 1) & (n == 6))
+            def _():
+                grad_stage_a()
+
+            @pl.when(far)
+            def _():
+                take_far(s, 2 * p)
+                take_far(s, 2 * p + 1)
+
+            split = (c == 0) | (bb == b)
+
+            @pl.when(split & (p == 0))
+            def _():
+                attend(s, bb, (0, 1), (0, 1))
+
+            @pl.when(split & (p == 1))
+            def _():
+                attend(s, bb, (2, 3), (2, 3))
+
+            @pl.when((c == 1) & (bb < b))
+            def _():
+                attend(s, bb, (2 * p, 2 * p + 1), (0, 0))
+
             return carry
 
-        lax.fori_loop(0, 4, drain, 0)
+        lax.fori_loop(0, 8, step, 0)
+        for r in range(4):
+            send_mix(s, r)
+
+        @pl.when(s == 0)
+        def _():
+            grad_partials()
+
+        return carry
+
+    cp_go.wait()
+    lax.fori_loop(0, 2, section, 0)
+    grad_stage_b()
+    states_ref[...] = (layer_norm(section_end(1)) * gain_ref[...]).astype(BF16)
+
+    for s in (0, 1):
+        for d in (1, 2, 3):
+            if d == 2:
+                kv_a(s, d).wait_send()
+            q_a(s, d).wait_send()
+            mix_a(s, d).wait_send()
+
+    def drain(n, carry):
+        s, r = n // 4, n % 4
+        for used, copy in (
+            (sends_r, hop_r), (sends_l, hop_l), (sends_v, hop_v),
+            (sends_far_k, far_k), (sends_far_kv, far_kv), (sends_far_v, far_v),
+        ):
+
+            @pl.when(used)
+            def _(copy=copy):
+                copy(s, r).wait_send()
+
+        return carry
+
+    lax.fori_loop(0, 8, drain, 0)
 
     for d in (1, 2, 3):
         gb[d - 1].wait_recv()
@@ -362,11 +508,12 @@
             buf(OWNED, DIM), buf(TOK, DIM), buf(2, DIM, 4 * DIM), buf(2, DIM, DIM),
             buf(4, 8, CAP, dtype=F32), buf(4, 8, CAP, dtype=F32),
             buf(4, CAP, DIM), buf(4, CAP, DIM), buf(4, CAP, DIM), buf(4, CAP, DIM),
-            buf(TOK, DIM), buf(4, 3, TOK, HD), buf(TOK, DIM),
+            buf(TOK, DIM), buf(2, 4, 3, TOK, HD), buf(TOK, DIM),
             buf(2, 4, 4, 2, TOK, HD), buf(2, 4, TOK, HD), buf(4, TOK, HD, dtype=F32),
-            buf(4, TOK, HD), buf(2, 4, TOK, HD),
+            buf(2, 4, TOK, HD), buf(2, 4, TOK, HD),
             buf(512, DIM), buf(512, DIM, dtype=F32), buf(512, DIM),
             buf(4, 128, DIM), buf(4, 128, DIM), buf(4, 32, DIM), buf(4, 32, DIM),
+            buf(4, TOK, HD), buf(4, 4, TOK, HD), buf(TOK, TOK, dtype=jnp.int32),
             pltpu.SemaphoreType.DMA((N_REMOTE,)),
             pltpu.SemaphoreType.DMA((N_REMOTE,)),
             pltpu.SemaphoreType.DMA((10,)),

time: 87.1 us -> 77.4 us (0.89)
  Pallas kernels: 83.1 us -> 72.6 us
    pallas_call x1, Pallas kernels: 83.1 us -> 72.6 us  [body(): pl.pallas_call(kernel, out_shape=(jax.ShapeDtypeStruct((TOK, DIM), BF16),...]
where the time goes in v2:
time: 77.4 us; the launch traced here: 76.4 us
  Pallas kernels  72.6 us (94%)
  local copies, waits for them, and re-layouts  3.14 us (4%)
    pallas_call x1, Pallas kernels, body(): pl.pallas_call(kernel, out_shape=(jax.ShapeDtypeStruct((TOK, DIM), BF16),...  72.6 us
    unnamed x2, local copies, waits for them, and re-layouts  3.14 us

profile of v2, /device:TPU:0, one launch (start us, length us, event | category | flops | bytes accessed | tf_op | source)
XLA Modules:
  0.0 76.4 jit_solution(809556862888906412)
XLA Ops:
  0.6 72.6 %shard_map.95 = (bf16[256,512]{1,0:T(8,128)(2,1)}, f32[32,512]{1,0:T(8,128)}) custom-call(s32[1,256]{1,0:T(1,128)} %bitcast.13, s32[1,256]{1,0:T(1,128)} %bitcast.14, s32[2,2]{1,0:T(2,128)} %bitcast.15, f32[1,512]{1,0:T(1,128)} %bitcast.12, bf16[1024,512]{1,0:T(8,128)(2,1)} %table_hbm.1, bf16[256,512]{1,0:T(8,128)(2,1)} %bitcast.10, ...), custom_call_target="tpu_custom_call" | custom-call | tf_op jit(solution)/shard_map/pallas_call | solution.py:499
  73.2 1.7 %copy.12 = bf16[1,1,256,512]{3,2,1,0:T(8,128)(2,1)} copy(bf16[1,1,256,512]{3,2,1,0:T(8,128)(2,1)} %bitcast.11) | data formatting | bytes 524288
  74.9 1.5 %copy.13 = f32[32,512]{1,0:T(8,128)} copy(f32[32,512]{1,0:T(8,128)} %get-tuple-element.9) | data formatting | bytes 131072

commit v3 on v2

--- a/solution.py
+++ b/solution.py
@@ -19,10 +19,14 @@
 CAP = 128
 OWNED = 1024
 
-KV_A, Q_A, HOP_R, HOP_L, FAR_K, FAR_V, MIX = 0, 3, 6, 10, 14, 18, 22
-PER_SECTION = 25
-REQ, ROWS, GRAD, WGT, OWGT, HALF, GA, GB = 50, 53, 56, 59, 60, 61, 62, 65
-N_REMOTE = 68
+KV_A, Q_A, HOP_R, HOP_L, FAR, MIX = 0, 3, 4, 8, 12, 16
+PER_SECTION = 17
+REQ, ROWS, GRAD, WGT, OWGT, HALF, GA, GB = 34, 37, 38, 39, 40, 41, 42, 43
+N_RECV = 44
+S_KV, _, S_Q, S_R, S_L, S_FK, S_FV, S_MIX = range(8)
+SENDS = 8
+S_REQ, S_ROWS, S_GRAD, S_WGT, S_OWGT, S_HALF, S_GA, S_GB = range(16, 24)
+N_SEND = 24
 
 
 def dot(left, right):
@@ -70,11 +74,14 @@
 
     other = {"phase": 1 - c}
 
-    def rc(src, dst, sem, dev):
+    def rc(src, dst, left, came, dev):
         return pltpu.make_async_remote_copy(
-            src_ref=src, dst_ref=dst, send_sem=ssem.at[sem], recv_sem=rsem.at[sem],
+            src_ref=src, dst_ref=dst, send_sem=ssem.at[left], recv_sem=rsem.at[came],
             device_id=dev, device_id_type=MESH,
         )
+
+    def all_of(ref, left, came):
+        return rc(ref, ref, left, came, other)
 
     cp_table = pltpu.make_async_copy(table_hbm, table, lsem.at[0])
     cp_grads = pltpu.make_async_copy(grads_hbm, grads, lsem.at[1])
@@ -116,11 +123,11 @@
             before = (pos + 256 * (sa * k + sb * h) < bound) & lane0
             k_ext[h, k] = jnp.where(before, 1.0, 0.0).astype(BF16)
     pl.semaphore_wait(barrier, 10)
-    req = [rc(req_snd.at[(ex + d) % 4], req_rcv.at[ex], REQ + d - 1, at_x(d)) for d in (1, 2, 3)]
+    req = [rc(req_snd.at[(ex + d) % 4], req_rcv.at[ex], S_REQ, REQ + d - 1, at_x(d)) for d in (1, 2, 3)]
     for d in (2, 1, 3):
         req[d - 1].start()
-    wgt = rc(w_hbm, w_all.at[c], WGT, other)
-    owgt = rc(ow_hbm, ow_all.at[c], OWGT, other)
+    wgt = rc(w_hbm, w_all.at[c], S_WGT, WGT, other)
+    owgt = rc(ow_hbm, ow_all.at[c], S_OWGT, OWGT, other)
     wgt.start()
     owgt.start()
 
@@ -142,7 +149,7 @@
         picked = (wanted == iota((CAP, OWNED), 1)).astype(F32).astype(BF16)
         rows_snd[q] = dot(picked, table[...]).astype(BF16)
 
-    rows = [rc(rows_snd.at[(ex + d) % 4], rows_rcv.at[ex], ROWS + d - 1, at_x(d)) for d in (1, 2, 3)]
+    rows = [rc(rows_snd.at[(ex + d) % 4], rows_rcv.at[ex], S_ROWS, ROWS, at_x(d)) for d in (1, 2, 3)]
     look_up(ex)
     cp_rows = pltpu.make_async_copy(rows_snd.at[ex], rows_rcv.at[ex], lsem.at[6])
     cp_rows.start()
@@ -151,14 +158,13 @@
         look_up((ex + 4 - d) % 4)
         rows[3 - d].start()
     cp_rows.wait()
-    for d in (1, 2, 3):
-        rows[d - 1].wait_recv()
+    all_of(rows_rcv.at[pl.ds(0, 3)], S_ROWS, ROWS).wait_recv()
     embedded = dot(
         place.astype(F32).astype(BF16), rows_rcv[...].reshape(4 * CAP, DIM)
     )
     x_ref[...] = embedded.astype(BF16)
 
-    grad = [rc(go_snd.at[(ex + d) % 4], g_rcv.at[ex], GRAD + d - 1, at_x(d)) for d in (1, 2, 3)]
+    grad = [rc(go_snd.at[(ex + d) % 4], g_rcv.at[ex], S_GRAD, GRAD, at_x(d)) for d in (1, 2, 3)]
     for d in (2, 1, 3):
         grad[d - 1].start()
     cp_w.wait()
@@ -177,42 +183,42 @@
             total = term if total is None else total + term
         return total
 
-    half = rc(half_snd, half_rcv, HALF, other)
-    ga = [rc(ga_snd.at[(a + d) % 4], ga_rcv.at[a], GA + d - 1, at_a(d)) for d in (1, 2, 3)]
-    gb = [rc(gb_snd.at[(b + d) % 4], gb_rcv.at[b], GB + d - 1, at_b(d)) for d in (1, 2, 3)]
+    half = rc(half_snd, half_rcv, S_HALF, HALF, other)
+    ga = [rc(ga_snd.at[(a + d) % 4], ga_rcv.at[a], S_GA, GA, at_a(d)) for d in (1, 2, 3)]
+    gb = [rc(gb_snd.at[(b + d) % 4], gb_rcv.at[b], S_GB, GB, at_b(d)) for d in (1, 2, 3)]
 
     def kv_a(s, d):
-        return rc(snd.at[s, (a + d) % 4, pl.ds(0, 2)], kv.at[s, b, a], s * PER_SECTION + KV_A + d - 1, at_a(d))
+        return rc(snd.at[s, (a + d) % 4, pl.ds(0, 2)], kv.at[s, b, a], s * SENDS + S_KV + 1 - d % 2, s * PER_SECTION + KV_A + d - 1, at_a(d))
 
     def q_a(s, d):
-        return rc(snd.at[s, (a + d) % 4, 2], qs.at[s, a], s * PER_SECTION + Q_A + d - 1, at_a(d))
+        return rc(snd.at[s, (a + d) % 4, 2], qs.at[s, a], s * SENDS + S_Q, s * PER_SECTION + Q_A, at_a(d))
 
     def mix_a(s, d):
-        return rc(mix_snd.at[s, (a + d) % 4], mix.at[s, a], s * PER_SECTION + MIX + d - 1, at_a(d))
+        return rc(mix_snd.at[s, (a + d) % 4], mix.at[s, a], s * SENDS + S_MIX, s * PER_SECTION + MIX, at_a(d))
 
     def hop_r(s, r):
         block = kv.at[s, b, r]
-        return rc(block, block, s * PER_SECTION + HOP_R + r, at_b(1))
+        return rc(block, block, s * SENDS + S_R, s * PER_SECTION + HOP_R + r, at_b(1))
 
     def hop_l(s, r):
         block = kv.at[s, b, r]
-        return rc(block, block, s * PER_SECTION + HOP_L + r, at_b(3))
+        return rc(block, block, s * SENDS + S_L, s * PER_SECTION + HOP_L + r, at_b(3))
 
     def hop_v(s, r):
         block = kv.at[s, b, r, 1]
-        return rc(block, block, s * PER_SECTION + HOP_L + r, at_b(3))
+        return rc(block, block, s * SENDS + S_L, s * PER_SECTION + HOP_L + r, at_b(3))
 
     def far_k(s, r):
         block = kv.at[s, (b + 3) % 4, r, 0]
-        return rc(block, block, s * PER_SECTION + FAR_K + r, at_b(1))
+        return rc(block, block, s * SENDS + S_FK, s * PER_SECTION + FAR + r, at_b(1))
 
     def far_kv(s, r):
         block = kv.at[s, (b + 3) % 4, r]
-        return rc(block, block, s * PER_SECTION + FAR_K + r, at_b(1))
+        return rc(block, block, s * SENDS + S_FK, s * PER_SECTION + FAR + r, at_b(1))
 
     def far_v(s, r):
         block = kv.at[s, (b + 1) % 4, r, 1]
-        return rc(block, block, s * PER_SECTION + FAR_V + r, at_b(3))
+        return rc(block, block, s * SENDS + S_FV, s * PER_SECTION + FAR + r, at_b(3))
 
     uses_l = (c == 0) | (b > 0)
     uses_r = (c == 0) | (b == 3)
@@ -265,8 +271,7 @@
     def take_far(s, r):
         @pl.when(uses_r)
         def _():
-            far_k(s, r).wait_recv()
-            far_v(s, r).wait_recv()
+            all_of(kv.at[s, b, r], s * SENDS + S_FK, s * PER_SECTION + FAR + r).wait_recv()
 
         @pl.when((c == 1) & (b == 2))
         def _():
@@ -297,15 +302,13 @@
         cp_q.start()
         gates[...] = silu(dot(normed, w_all[s, :, 0:DIM])).astype(BF16)
         cp_q.wait()
-        kv_a(s, 1).wait_send()
-        kv_a(s, 3).wait_send()
-        kv_a(s, 2).start()
+        all_of(kv.at[s, b, pl.ds(0, 2)], s * SENDS + S_KV, 0).wait_send()
         for d in (1, 3, 2):
             q_a(s, d).start()
+        kv_a(s, 2).start()
 
     def section_end(s):
-        for d in (1, 2, 3):
-            mix_a(s, d).wait_recv()
+        all_of(mix.at[s, pl.ds(0, 3)], s * SENDS + S_MIX, s * PER_SECTION + MIX).wait_recv()
         mixed = jnp.concatenate([mix[s, h] for h in range(4)], axis=1).astype(F32)
         gated = (layer_norm(mixed) * gates[...].astype(F32)).astype(BF16)
         return x_ref[...].astype(F32) + dot(gated, ow_all[s])
@@ -320,31 +323,33 @@
             mix_snd[s, r] = acc[r].astype(BF16)
             mix_a(s, (r + 4 - a) % 4).start()
 
-    def attend(s, bb, rows, firsts):
-        terms = []
-        for r, first in zip(rows, firsts):
+    def attend(s, first, blocks):
+        m = (4 - first) * TOK
+        queries = jnp.concatenate(
+            [qs[s, first:4].reshape(m, HD), q_ext[first:4].reshape(m, HD)], axis=1
+        )
+        total = None
+        for bb, r, masked in blocks:
             keys = jnp.concatenate([kv[s, bb, r, 0], k_ext[bb, r]], axis=1)
-            m = (4 - first) * TOK
-            queries = jnp.concatenate(
-                [qs[s, first:4].reshape(m, HD), q_ext[first:4].reshape(m, HD)], axis=1
-            )
             u = lax.dot_general(
                 queries, keys, (((1,), (1,)), ((), ())), preferred_element_type=F32
             )
             weights = u + u * jnp.tanh(u)
-            ahead = 256 * (sa * r + sb * bb) - 256 * (sa * first + sb * b)
-            head = jnp.where(diff_ref[...] >= ahead, weights[:TOK], 0.0)
-            weights = jnp.concatenate([head, weights[TOK:]], axis=0) if first < 3 else head
-            terms.append(dot(weights.astype(BF16), kv[s, bb, r, 1]))
-        low, high = firsts
-        apart = (high - low) * TOK
-        if apart:
-            acc[low:high] += terms[0][:apart].reshape(high - low, TOK, HD)
-        acc[high:4] += (terms[0][apart:] + terms[1]).reshape(4 - high, TOK, HD)
+            parts = []
+            for k in range(masked):
+                ahead = 256 * (sa * r + sb * bb) - 256 * (sa * (first + k) + sb * b)
+                part = weights[k * TOK : (k + 1) * TOK]
+                parts.append(jnp.where(diff_ref[...] >= ahead, part, 0.0))
+            if masked:
+                if first + masked < 4:
+                    parts.append(weights[masked * TOK :])
+                weights = jnp.concatenate(parts, axis=0)
+            term = dot(weights.astype(BF16), kv[s, bb, r, 1])
+            total = term if total is None else total + term
+        acc[first:4] += total.reshape(4 - first, TOK, HD)
 
     def grad_partials():
-        for d in (1, 2, 3):
-            grad[d - 1].wait_recv()
+        all_of(g_rcv.at[pl.ds(0, 3)], S_GRAD, GRAD).wait_recv()
         half_snd[...] = partial_half(1 - c).astype(BF16)
         half.start()
         half_own[...] = partial_half(c)
@@ -359,8 +364,7 @@
             ga[d - 1].start()
 
     def grad_stage_b():
-        for d in (1, 2, 3):
-            ga[d - 1].wait_recv()
+        all_of(ga_rcv.at[pl.ds(0, 3)], S_GA, GA).wait_recv()
         total = half_own[pl.ds(pl.multiple_of(a * 128, 128), 128), :]
         for d in (1, 2, 3):
             total = total + ga_rcv[(a + d) % 4].astype(F32)
@@ -377,69 +381,77 @@
 
         section_start(s)
         acc[...] = jnp.zeros_like(acc)
-        for d in (1, 3, 2):
+        odd = a % 2
+        pair = a // 2
+        mate, next_row, last_row = a + 1 - 2 * odd, (a + 3 + 2 * odd) % 4, (a + 2) % 4
+        for d in (3 - 2 * odd, 1 + 2 * odd):
             kv_a(s, d).wait_recv()
 
             @pl.when(c == 0)
             def _(d=d):
                 start_hops(s, (a + 4 - d) % 4)
 
+        @pl.when(c == 0)
+        def _():
+            take_left(s, a)
+            take_right(s, a)
+
+        all_of(qs.at[s, pl.ds(0, 3)], s * SENDS + S_Q, s * PER_SECTION + Q_A).wait_recv()
+
         @pl.when(c == 1)
         def _():
-            for d in (0, 1, 3, 2):
-                start_hops(s, (a + 4 - d) % 4)
-
-        for d in (1, 3, 2):
-            q_a(s, d).wait_recv()
-
-        take_left(s, a)
-        take_right(s, a)
-
-        def take_pair(take, p):
-            for k in (0, 1):
-
-                @pl.when(2 * p + k != a)
-                def _(k=k):
-                    take(s, 2 * p + k)
-
-        def step(n, carry):
-            own, far = n < 2, n >= 6
-            side = n % 2
-            p = jnp.where(own, n, jnp.where(far, n - 6, (n - 2) // 2))
-            bb = (b + jnp.where(own, 0, jnp.where(far, 2, 3 - 2 * side))) % 4
-            near = (n >= 2) & (n < 6)
-
-            @pl.when(near & (side == 0))
-            def _():
-                take_pair(take_left, p)
-                take_pair(take_right, p)
-
-            @pl.when((s == 1) & (n == 6))
-            def _():
-                grad_stage_a()
-
-            @pl.when(far)
-            def _():
+            for r in (a, mate, next_row):
+                start_hops(s, r)
+
+        kv_a(s, 2).wait_recv()
+        start_hops(s, last_row)
+
+        takes = {
+            0: ((0, mate),),
+            1: ((0, next_row), (1, a)),
+            2: ((1, mate),),
+            3: ((0, last_row), (1, next_row)),
+            4: ((1, last_row),),
+        }
+        for n, (kind, second) in enumerate(
+            ((0, 0), (0, 1), (1, 0), (2, 0), (1, 1), (2, 1), (3, 0), (3, 1))
+        ):
+            p = 1 - pair if second else pair
+            bb = (b + (0, 3, 1, 2)[kind]) % 4
+
+            for core, r in takes.get(n, ()):
+
+                @pl.when(c == core)
+                def _(r=r):
+                    take_left(s, r)
+                    take_right(s, r)
+
+            if n in (0, 2):
+
+                @pl.when((s == 1) & (c == 1 - n // 2))
+                def _():
+                    grad_stage_a()
+
+            if kind == 3:
                 take_far(s, 2 * p)
                 take_far(s, 2 * p + 1)
 
-            split = (c == 0) | (bb == b)
+            split = (p >= 0) if kind == 0 else (c == 0)
 
             @pl.when(split & (p == 0))
-            def _():
-                attend(s, bb, (0, 1), (0, 1))
+            def _(bb=bb):
+                attend(s, 0, ((bb, 0, 1), (bb, 1, 2)))
 
             @pl.when(split & (p == 1))
-            def _():
-                attend(s, bb, (2, 3), (2, 3))
-
-            @pl.when((c == 1) & (bb < b))
-            def _():
-                attend(s, bb, (2 * p, 2 * p + 1), (0, 0))
-
-            return carry
-
-        lax.fori_loop(0, 8, step, 0)
+            def _(bb=bb):
+                attend(s, 2, ((bb, 2, 1), (bb, 3, 2)))
+
+            if kind:
+
+                @pl.when((c == 1) & (bb < b))
+                def _(bb=bb, p=p):
+                    attend(s, 0, ((bb, 2 * p, 0), (bb, 2 * p + 1, 0)))
+
         for r in range(4):
             send_mix(s, r)
 
@@ -455,34 +467,29 @@
     states_ref[...] = (layer_norm(section_end(1)) * gain_ref[...]).astype(BF16)
 
     for s in (0, 1):
-        for d in (1, 2, 3):
-            if d == 2:
-                kv_a(s, d).wait_send()
-            q_a(s, d).wait_send()
-            mix_a(s, d).wait_send()
-
-    def drain(n, carry):
-        s, r = n // 4, n % 4
-        for used, copy in (
-            (sends_r, hop_r), (sends_l, hop_l), (sends_v, hop_v),
-            (sends_far_k, far_k), (sends_far_kv, far_kv), (sends_far_v, far_v),
+        kv_a(s, 2).wait_send()
+        all_of(qs.at[s, pl.ds(0, 3)], s * SENDS + S_Q, 0).wait_send()
+        all_of(mix.at[s, pl.ds(0, 3)], s * SENDS + S_MIX, 0).wait_send()
+        whole, part = kv.at[s, b], kv.at[s, b, pl.ds(0, 2)]
+        for used, ref, left in (
+            (sends_r, whole, S_R), (sends_l, whole, S_L), (sends_v, part, S_L),
+            (sends_far_k, part, S_FK), (sends_far_kv, whole, S_FK), (sends_far_v, part, S_FV),
         ):
 
             @pl.when(used)
-            def _(copy=copy):
-                copy(s, r).wait_send()
-
-        return carry
-
-    lax.fori_loop(0, 8, drain, 0)
-
-    for d in (1, 2, 3):
-        gb[d - 1].wait_recv()
+            def _(ref=ref, left=left, s=s):
+                all_of(ref, s * SENDS + left, 0).wait_send()
+
+    all_of(gb_rcv.at[pl.ds(0, 3)], S_GB, GB).wait_recv()
     total = half_own[pl.ds(pl.multiple_of(b * 32, 32), 32), :]
     for d in (1, 2, 3):
         total = total + gb_rcv[(b + d) % 4].astype(F32)
     tg_ref[...] = total
-    for cp in req + rows + grad + [wgt, owgt, half] + ga + gb:
+    for ref, left in (
+        (req_rcv, S_REQ), (rows_rcv, S_ROWS), (g_rcv, S_GRAD), (ga_rcv, S_GA), (gb_rcv, S_GB),
+    ):
+        all_of(ref.at[pl.ds(0, 3)], left, 0).wait_send()
+    for cp in (wgt, owgt, half):
         cp.wait_send()
 
 
@@ -514,8 +521,8 @@
             buf(512, DIM), buf(512, DIM, dtype=F32), buf(512, DIM),
             buf(4, 128, DIM), buf(4, 128, DIM), buf(4, 32, DIM), buf(4, 32, DIM),
             buf(4, TOK, HD), buf(4, 4, TOK, HD), buf(TOK, TOK, dtype=jnp.int32),
-            pltpu.SemaphoreType.DMA((N_REMOTE,)),
-            pltpu.SemaphoreType.DMA((N_REMOTE,)),
+            pltpu.SemaphoreType.DMA((N_SEND,)),
+            pltpu.SemaphoreType.DMA((N_RECV,)),
             pltpu.SemaphoreType.DMA((10,)),
         ],
         compiler_params=pltpu.CompilerParams(
@@ -531,6 +538,19 @@
         proj_weight.reshape(DIM, 4 * DIM),
         out_weight.reshape(DIM, DIM),
     )
+    def hand_out(states_in, grad_in, states_out, grad_out):
+        states_out[...] = states_in[...]
+        grad_out[...] = grad_in[...]
+
+    states, table_grad = pl.pallas_call(
+        hand_out,
+        out_shape=(
+            jax.ShapeDtypeStruct((TOK, DIM), BF16),
+            jax.ShapeDtypeStruct((32, DIM), F32),
+        ),
+        in_specs=[vmem, vmem],
+        out_specs=(vmem, vmem),
+    )(states, table_grad)
     return states.reshape(1, 1, TOK, DIM), table_grad
 
 

time: 77.4 us -> 73.8 us (0.953)
  local copies, waits for them, and re-layouts: 3.14 us -> 0 us
    unnamed x2 -> x0, local copies, waits for them, and re-layouts: 3.14 us -> none
    pallas_call x0 -> x1, Pallas kernels: none -> 1.69 us  [body(): pl.pallas_call(hand_out, out_shape=(jax.ShapeDtypeStruct((TOK, DIM), BF16...]
    pallas_call x1, Pallas kernels: 72.6 us -> 71 us  [body(): pl.pallas_call(kernel, out_shape=(jax.ShapeDtypeStruct((TOK, DIM), BF16),...]
where the time goes in v3:
time: 73.8 us; the launch traced here: 73.3 us
  Pallas kernels  72.7 us (99%)
    pallas_call x1, Pallas kernels, body(): pl.pallas_call(kernel, out_shape=(jax.ShapeDtypeStruct((TOK, DIM), BF16),...  71 us
    pallas_call x1, Pallas kernels, body(): pl.pallas_call(hand_out, out_shape=(jax.ShapeDtypeStruct((TOK, DIM), BF16...  1.69 us

profile of v3, /device:TPU:0, one launch (start us, length us, event | category | flops | bytes accessed | tf_op | source)
XLA Modules:
  0.0 73.3 jit_solution(2422457031471849011)
XLA Ops:
  0.6 71.0 %shard_map.95 = (bf16[256,512]{1,0:T(8,128)(2,1)}, f32[32,512]{1,0:T(8,128)}) custom-call(s32[1,256]{1,0:T(1,128)} %bitcast.12, s32[1,256]{1,0:T(1,128)} %bitcast.13, s32[2,2]{1,0:T(2,128)} %bitcast.14, f32[1,512]{1,0:T(1,128)} %bitcast.11, bf16[1024,512]{1,0:T(8,128)(2,1)} %table_hbm.1, bf16[256,512]{1,0:T(8,128)(2,1)} %bitcast.10, ...), custom_call_target="tpu_custom_call" | custom-call | tf_op jit(solution)/shard_map/pallas_call | solution.py:506
  71.6 1.7 %shard_map.96 = (bf16[256,512]{1,0:T(8,128)(2,1)}, f32[32,512]{1,0:T(8,128)}) custom-call(bf16[256,512]{1,0:T(8,128)(2,1)} %get-tuple-element.6.states_in, f32[32,512]{1,0:T(8,128)} %get-tuple-element.7.grad_in), custom_call_target="tpu_custom_call" | custom-call | tf_op jit(solution)/shard_map/pallas_call | solution.py:545

commit v4 on v3

--- a/solution.py
+++ b/solution.py
@@ -49,9 +49,9 @@
 
 
 def kernel(
-    owner_ref, slot_ref, len_ref, gain_ref, table_hbm, grads_hbm, w_hbm, ow_hbm,
+    owner_hbm, slot_hbm, len_hbm, gain_hbm, table_hbm, grads_hbm, w_hbm, ow_hbm,
     states_ref, tg_ref,
-    table, grads, w_all, ow_all, req_snd, req_rcv, rows_snd, rows_rcv, go_snd, g_rcv,
+    owner_ref, slot_ref, len_ref, gain_ref, table, grads, w_all, ow_all, req_snd, req_rcv, rows_snd, rows_rcv, go_snd, g_rcv,
     x_ref, snd, gates, kv, qs, acc, mix_snd, mix, half_snd, half_own, half_rcv,
     ga_snd, ga_rcv, gb_snd, gb_rcv, q_ext, k_ext, diff_ref, ssem, rsem, lsem,
 ):
@@ -83,17 +83,30 @@
     def all_of(ref, left, came):
         return rc(ref, ref, left, came, other)
 
+    barrier = pltpu.get_barrier_semaphore()
+    for d in (1, 2, 3):
+        for dev in (at_x(d), at_a(d), at_b(d)):
+            pl.semaphore_signal(barrier, inc=1, device_id=dev, device_id_type=MESH)
+    pl.semaphore_signal(barrier, inc=1, device_id=other, device_id_type=MESH)
+    small = [
+        pltpu.make_async_copy(src, dst, lsem.at[4 + k])
+        for k, (src, dst) in enumerate(
+            (
+                (owner_hbm, owner_ref), (slot_hbm, slot_ref), (len_hbm, len_ref),
+                (gain_hbm, gain_ref),
+            )
+        )
+    ]
+    for cp in small:
+        cp.start()
     cp_table = pltpu.make_async_copy(table_hbm, table, lsem.at[0])
     cp_grads = pltpu.make_async_copy(grads_hbm, grads, lsem.at[1])
     cp_w = pltpu.make_async_copy(w_hbm, w_all.at[c], lsem.at[2])
     cp_ow = pltpu.make_async_copy(ow_hbm, ow_all.at[c], lsem.at[3])
     for cp in (cp_table, cp_grads, cp_w, cp_ow):
         cp.start()
-    barrier = pltpu.get_barrier_semaphore()
-    for d in (1, 2, 3):
-        for dev in (at_x(d), at_a(d), at_b(d)):
-            pl.semaphore_signal(barrier, inc=1, device_id=dev, device_id_type=MESH)
-    pl.semaphore_signal(barrier, inc=1, device_id=other, device_id_type=MESH)
+    for cp in small:
+        cp.wait()
 
     own_row = owner_ref[...].astype(F32)
     slot_row = slot_ref[...].astype(F32)
@@ -289,13 +302,16 @@
         project(1, 512, 1.0)
         for d in (1, 3):
             kv_a(s, d).start()
+
+        @pl.when(c == 0)
+        def _():
+            kv_a(s, 2).start()
+
         cp_kv = pltpu.make_async_copy(snd.at[s, a, pl.ds(0, 2)], kv.at[s, b, a], lsem.at[7])
         cp_kv.start()
         cp_kv.wait()
 
-        @pl.when(c == 0)
-        def _():
-            start_hops(s, a)
+        start_hops(s, a)
 
         project(2, 1024, 0.5)
         cp_q = pltpu.make_async_copy(snd.at[s, a, 2], qs.at[s, a], lsem.at[8])
@@ -305,7 +321,10 @@
         all_of(kv.at[s, b, pl.ds(0, 2)], s * SENDS + S_KV, 0).wait_send()
         for d in (1, 3, 2):
             q_a(s, d).start()
-        kv_a(s, 2).start()
+
+        @pl.when(c == 1)
+        def _():
+            kv_a(s, 2).start()
 
     def section_end(s):
         all_of(mix.at[s, pl.ds(0, 3)], s * SENDS + S_MIX, s * PER_SECTION + MIX).wait_recv()
@@ -393,6 +412,8 @@
 
         @pl.when(c == 0)
         def _():
+            kv_a(s, 2).wait_recv()
+            start_hops(s, last_row)
             take_left(s, a)
             take_right(s, a)
 
@@ -400,11 +421,13 @@
 
         @pl.when(c == 1)
         def _():
-            for r in (a, mate, next_row):
+            for r in (mate, next_row):
                 start_hops(s, r)
 
-        kv_a(s, 2).wait_recv()
-        start_hops(s, last_row)
+        @pl.when(c == 1)
+        def _():
+            kv_a(s, 2).wait_recv()
+            start_hops(s, last_row)
 
         takes = {
             0: ((0, mate),),
@@ -498,7 +521,6 @@
 ):
     vmem = pl.BlockSpec(memory_space=pltpu.VMEM)
     hbm = pl.BlockSpec(memory_space=pl.ANY)
-    smem = pl.BlockSpec(memory_space=pltpu.SMEM)
 
     def buf(*shape, dtype=BF16):
         return pltpu.VMEM(shape, dtype)
@@ -509,9 +531,11 @@
             jax.ShapeDtypeStruct((TOK, DIM), BF16),
             jax.ShapeDtypeStruct((32, DIM), F32),
         ),
-        in_specs=[vmem, vmem, smem, vmem, hbm, hbm, hbm, hbm],
+        in_specs=[hbm] * 8,
         out_specs=(vmem, vmem),
         scratch_shapes=[
+            buf(1, TOK, dtype=jnp.int32), buf(1, TOK, dtype=jnp.int32),
+            pltpu.SMEM((2, 2), jnp.int32), buf(1, DIM, dtype=F32),
             buf(OWNED, DIM), buf(TOK, DIM), buf(2, DIM, 4 * DIM), buf(2, DIM, DIM),
             buf(4, 8, CAP, dtype=F32), buf(4, 8, CAP, dtype=F32),
             buf(4, CAP, DIM), buf(4, CAP, DIM), buf(4, CAP, DIM), buf(4, CAP, DIM),

time: 73.8 us -> 69.6 us (0.943)
  Pallas kernels: 72.7 us -> 68.9 us
    pallas_call x1, Pallas kernels: 71 us -> 67.2 us  [body(): pl.pallas_call(kernel, out_shape=(jax.ShapeDtypeStruct((TOK, DIM), BF16),...]
where the time goes in v4:
time: 69.6 us; the launch traced here: 69.5 us
  Pallas kernels  68.9 us (99%)
    pallas_call x1, Pallas kernels, body(): pl.pallas_call(kernel, out_shape=(jax.ShapeDtypeStruct((TOK, DIM), BF16),...  67.2 us
    pallas_call x1, Pallas kernels, body(): pl.pallas_call(hand_out, out_shape=(jax.ShapeDtypeStruct((TOK, DIM), BF16...  1.69 us

profile of v4, /device:TPU:0, one launch (start us, length us, event | category | flops | bytes accessed | tf_op | source)
XLA Modules:
  0.0 69.5 jit_solution(10520464540874542511)
XLA Ops:
  0.6 67.2 %shard_map.95 = (bf16[256,512]{1,0:T(8,128)(2,1)}, f32[32,512]{1,0:T(8,128)}) custom-call(s32[1,256]{1,0:T(1,128)} %bitcast.12, s32[1,256]{1,0:T(1,128)} %bitcast.13, s32[2,2]{1,0:T(2,128)} %bitcast.14, f32[1,512]{1,0:T(1,128)} %bitcast.11, bf16[1024,512]{1,0:T(8,128)(2,1)} %table_hbm.1, bf16[256,512]{1,0:T(8,128)(2,1)} %bitcast.10, ...), custom_call_target="tpu_custom_call" | custom-call | tf_op jit(solution)/shard_map/pallas_call | solution.py:528
  67.8 1.7 %shard_map.96 = (bf16[256,512]{1,0:T(8,128)(2,1)}, f32[32,512]{1,0:T(8,128)}) custom-call(bf16[256,512]{1,0:T(8,128)(2,1)} %get-tuple-element.6.states_in, f32[32,512]{1,0:T(8,128)} %get-tuple-element.7.grad_in), custom_call_target="tpu_custom_call" | custom-call | tf_op jit(solution)/shard_map/pallas_call | solution.py:569

commit v5 on v4

--- a/solution.py
+++ b/solution.py
@@ -432,8 +432,8 @@
         takes = {
             0: ((0, mate),),
             1: ((0, next_row), (1, a)),
-            2: ((1, mate),),
-            3: ((0, last_row), (1, next_row)),
+            2: ((0, last_row), (1, mate)),
+            3: ((1, next_row),),
             4: ((1, last_row),),
         }
         for n, (kind, second) in enumerate(

time: 69.6 us -> 70 us (level)
  no operation moved by 1% of the time
where the time goes in v5:
time: 70 us; the launch traced here: 69.8 us
  Pallas kernels  69.2 us (99%)
    pallas_call x1, Pallas kernels, body(): pl.pallas_call(kernel, out_shape=(jax.ShapeDtypeStruct((TOK, DIM), BF16),...  67.5 us
    pallas_call x1, Pallas kernels, body(): pl.pallas_call(hand_out, out_shape=(jax.ShapeDtypeStruct((TOK, DIM), BF16...  1.69 us

profile of v5, /device:TPU:0, one launch (start us, length us, event | category | flops | bytes accessed | tf_op | source)
XLA Modules:
  0.0 69.8 jit_solution(3155179065640719027)
XLA Ops:
  0.6 67.5 %shard_map.95 = (bf16[256,512]{1,0:T(8,128)(2,1)}, f32[32,512]{1,0:T(8,128)}) custom-call(s32[1,256]{1,0:T(1,128)} %bitcast.12, s32[1,256]{1,0:T(1,128)} %bitcast.13, s32[2,2]{1,0:T(2,128)} %bitcast.14, f32[1,512]{1,0:T(1,128)} %bitcast.11, bf16[1024,512]{1,0:T(8,128)(2,1)} %table_hbm.1, bf16[256,512]{1,0:T(8,128)(2,1)} %bitcast.10, ...), custom_call_target="tpu_custom_call" | custom-call | tf_op jit(solution)/shard_map/pallas_call | solution.py:528
  68.2 1.7 %shard_map.96 = (bf16[256,512]{1,0:T(8,128)(2,1)}, f32[32,512]{1,0:T(8,128)}) custom-call(bf16[256,512]{1,0:T(8,128)(2,1)} %get-tuple-element.6.states_in, f32[32,512]{1,0:T(8,128)} %get-tuple-element.7.grad_in), custom_call_target="tpu_custom_call" | custom-call | tf_op jit(solution)/shard_map/pallas_call | solution.py:569
